TPU v7x, 32 devices: a whole 2x2x4 slice. The times are simulated.
32 devices in a mesh: node: 8 (over z, x), rep: 4 (over y, core).
Axes of the slice: x: 2, y: 2, z: 4, core: 2. Of those that a mesh axis runs over, the one named last changes fastest.
Arguments:
- features: bfloat16 [8192, 512], P(('node', 'rep')), may hold values from -6 to 6
- weight: bfloat16 [512, 512], replicated, may hold values from -0.25 to 0.25
- cotangent: bfloat16 [8192, 512], P(('node', 'rep')), may hold values from -6 to 6
- tile_values: bfloat16 [8192, 128, 128], P(('node', 'rep')), may hold values from -0.125 to 0.125
- tile_row: int32 [8192], P(('node', 'rep')), may hold values from 0 to 7
- tile_col: int32 [8192], P(('node', 'rep')), may hold values from 0 to 15
- tile_count: int32 [32], P(('node', 'rep')), may hold values from 64 to 256, as said below
Outputs:
- activation: bfloat16 [8192, 512], P(('node', 'rep'))
- weight_grad: float32 [512, 512], replicated
- feature_grad: bfloat16 [8192, 512], P(('node', 'rep'))
Inputs may be any that keep to these rules, and one draw needn't show every extreme that they name: `tile_count`: slots of a device below its count hold tiles, the others are ignored; some device uses all 256 slots.
All inputs are finite; a program needn't handle non-finite values.
Results may differ from a plain program's by a relative error of at most 0.023.
Values may be sent and summed in bfloat16 or wider, within the bound.
A program may use at most 128 MiB of HBM per device.

v0:
```python
import functools
import math

import jax
import jax.numpy as jnp
from jax import lax
from jax.experimental import pallas as pl
from jax.experimental.pallas import tpu as pltpu
from jax.sharding import PartitionSpec as P

TB = 128


def densify_kernel(blocks, subs, group, rows_ref, cols_ref, count_ref, tiles_ref, out_ref, acc, stage, sems):
    turn = pl.program_id(0)
    places = acc.shape[0] - 1
    nodes = places // (blocks * subs)

    @pl.when(turn == 0)
    def _():
        @pl.loop(0, places)
        def _(p):
            acc[p] = jnp.zeros((TB, TB), jnp.float32)

    count = count_ref[0]

    @pl.when(turn * group < count)
    def _():
        for t in range(group):
            slot = turn * group + t
            col = cols_ref[slot]
            place = (col // subs * blocks + rows_ref[slot]) * subs + col % subs
            place = jnp.where(slot < count, place, places)
            acc[place] += tiles_ref[t].astype(jnp.float32)

    @pl.when(turn == pl.num_programs(0) - 1)
    def _():
        def copy_out(o):
            return pltpu.make_async_copy(stage.at[o % 2], out_ref.at[o], sems.at[o % 2])

        for o in range(nodes):
            if o >= 2:
                copy_out(o - 2).wait()
            for r in range(blocks):
                for s in range(subs):
                    stage[o % 2, r * TB:(r + 1) * TB, s * TB:(s + 1) * TB] = acc[
                        (o * blocks + r) * subs + s
                    ].astype(jnp.bfloat16)
            copy_out(o).start()
        for o in range(max(nodes - 2, 0), nodes):
            copy_out(o).wait()


def densify(tile_values, tile_row, tile_col, tile_count, nodes, blocks, subs):
    slots = tile_values.shape[0]
    group = 16 if slots % 16 == 0 else 1
    places = nodes * blocks * subs

    def tile_block(i, rows, cols, count):
        return (jnp.minimum(i, (count[0] + group - 1) // group - 1), 0, 0)

    return pl.pallas_call(
        functools.partial(densify_kernel, blocks, subs, group),
        out_shape=jax.ShapeDtypeStruct((nodes, blocks * TB, subs * TB), jnp.bfloat16),
        grid_spec=pltpu.PrefetchScalarGridSpec(
            num_scalar_prefetch=3,
            grid=(slots // group,),
            in_specs=[pl.BlockSpec((group, TB, TB), tile_block)],
            out_specs=pl.BlockSpec(memory_space=pl.ANY),
            scratch_shapes=[
                pltpu.VMEM((places + 1, TB, TB), jnp.float32),
                pltpu.VMEM((2, blocks * TB, subs * TB), jnp.bfloat16),
                pltpu.SemaphoreType.DMA((2,)),
            ],
        ),
        compiler_params=pltpu.CompilerParams(vmem_limit_bytes=60 * 1024 * 1024),
        name="densify",
    )(tile_row, tile_col, tile_count, tile_values)


def local(features, weight, cotangent, tile_values, tile_row, tile_col, tile_count):
    rows_quarter, width = features.shape
    rep_count = lax.axis_size("rep")
    node_count = lax.axis_size("node")
    scale = 1.0 / math.sqrt(rows_quarter * rep_count * node_count)
    subs = rows_quarter // TB
    blocks = subs * rep_count
    dense = densify(tile_values, tile_row, tile_col, tile_count, node_count, blocks, subs)
    gathered = lax.all_gather(features, "node", axis=0, tiled=False)
    partial_sum = lax.dot_general(
        dense, gathered, (((0, 2), (0, 1)), ((), ())), preferred_element_type=jnp.float32
    )
    aggregate = lax.psum_scatter(
        partial_sum.astype(jnp.bfloat16), "rep", scatter_dimension=0, tiled=True
    )
    pre = jnp.dot(aggregate, weight, preferred_element_type=jnp.float32)
    activated, pullback = jax.vjp(functools.partial(jax.nn.gelu, approximate=True), pre)
    pre_grad = pullback(cotangent.astype(jnp.float32))[0].astype(jnp.bfloat16)
    row_grad = jnp.dot(pre_grad, weight.T, preferred_element_type=jnp.float32).astype(jnp.bfloat16)
    all_grad = lax.all_gather(row_grad, "rep", axis=0, tiled=True)
    weight_term = jnp.dot(aggregate.T, pre_grad, preferred_element_type=jnp.float32)
    weight_grad = lax.psum(weight_term, ("node", "rep")) * scale
    terms = lax.dot_general(
        dense, all_grad, (((1,), (0,)), ((), ())), preferred_element_type=jnp.float32
    ).astype(jnp.bfloat16)
    feature_grad = lax.psum_scatter(
        terms.reshape(-1, width), "node", scatter_dimension=0, tiled=True
    )
    return (activated.astype(jnp.bfloat16), weight_grad, feature_grad)


def solution(mesh):
    in_specs = (
        P(("node", "rep"), None),
        P(),
        P(("node", "rep"), None),
        P(("node", "rep"), None, None),
        P(("node", "rep")),
        P(("node", "rep")),
        P(("node", "rep")),
    )
    out_specs = (P(("node", "rep"), None), P(), P(("node", "rep"), None))
    return jax.shard_map(local, mesh=mesh, in_specs=in_specs, out_specs=out_specs, check_vma=False)
```

profile of v0, /device:TPU:0, one launch (start us, length us, event | category | flops | bytes accessed | tf_op | source)
XLA Modules:
  0.0 325.9 jit_solution(5693229874085195882)
XLA Ops:
  7.2 0.0 copy-start
  7.2 0.0 all-gather.6.cloned.1.call-start
  7.2 0.7 all-gather.6.cloned.1.call-update
  7.9 0.0 reduce-scatter.3.cloned.1.call-start
  8.6 9.2 %densify.1 = bf16[8,1024,256]{2,1,0:T(8,128)(2,1)} custom-call(s32[256]{0:T(256)} %rows_ref.1, s32[256]{0:T(256)} %cols_ref.1, s32[1]{0:T(128)S(6)} %copy.13.count_ref, bf16[256,128,128]{2,1,0:T(8,128)(2,1)} %tiles_ref.1), custom_call_target="tpu_custom_call" | custom-call | tf_op jit(solution)/shard_map/densify/pallas_call | solution.py:62
  17.8 44.2 %all-gather.6.cloned.1.call-done = bf16[2048,512]{1,0:T(8,128)(2,1)} async-done(((bf16[256,512]{1,0:T(8,128)(2,1)}), bf16[2048,512]{1,0:T(8,128)(2,1)}) %all-gather.6.cloned.1.call-update) | async-done | bytes 2097168 | tf_op jit(solution)/shard_map/all_gather | solution.py:89
  62.0 0.0 copy-start.2
  62.0 6.2 %bitcast_convert_fusion = bf16[1024,512]{1,0:T(8,128)(2,1)} fusion(bf16[8,1024,256]{2,1,0:T(8,128)(2,1)} %densify.1, bf16[8,256,512]{2,1,0:T(8,128)(2,1)} %bitcast.17), kind=kOutput, calls=%fused_computation | convolution fusion | flops 2148007936 | bytes 7340032 | tf_op jit(solution)/shard_map/dot_general | solution.py:90
  68.2 0.0 reduce-scatter.3.cloned.1.call-update
  68.2 0.0 all-gather.4.cloned.1.call-start
  68.2 23.4 %reduce-scatter.3.cloned.1.call-done = bf16[256,512]{1,0:T(8,128)(2,1)} async-done(((bf16[1024,512]{1,0:T(8,128)(2,1)}), bf16[256,512]{1,0:T(8,128)(2,1)}) %reduce-scatter.3.cloned.1.call-update) | async-done | bytes 262160 | tf_op jit(solution)/shard_map/reduce_scatter | solution.py:93
  91.7 0.0 copy-done
  91.7 0.0 copy-done.2
  91.7 0.0 copy-start.1
  91.7 2.4 fusion.3
  94.0 1.0 convolution_convert_fusion.1
  95.1 0.0 all-gather.4.cloned.1.call-update
  95.1 0.0 all-reduce.2.cloned.1.call-start
  95.1 0.0 copy-done.1
  95.2 1.3 fusion.11
  96.5 0.0 all-reduce.2.cloned.1.call-update
  96.5 0.0 reduce-scatter.5.cloned.1.call-start
  96.5 15.4 %all-gather.4.cloned.1.call-done = bf16[1024,512]{1,0:T(8,128)(2,1)} async-done(((bf16[256,512]{1,0:T(8,128)(2,1)}), bf16[1024,512]{1,0:T(8,128)(2,1)}) %all-gather.4.cloned.1.call-update) | async-done | bytes 1048592 | tf_op jit(solution)/shard_map/all_gather | solution.py:100
  112.0 6.2 %convolution_convert_fusion = bf16[8,256,512]{2,1,0:T(8,128)(2,1)} fusion(bf16[8,1024,256]{2,1,0:T(8,128)(2,1)} %densify.1, bf16[1024,512]{1,0:T(8,128)(2,1)} %all-gather.4.cloned.1.call-done), kind=kOutput, calls=%fused_computation.1 | convolution fusion | flops 2148532224 | bytes 7340032 | tf_op jit(solution)/shard_map/dot_general | solution.py:103
  118.1 0.0 reduce-scatter.5.cloned.1.call-update
  118.2 130.1 %all-reduce.2.cloned.1.call-done = f32[512,512]{1,0:T(8,128)} async-done(((f32[512,512]{1,0:T(8,128)}), f32[512,512]{1,0:T(8,128)}) %all-reduce.2.cloned.1.call-update) | async-done | bytes 1048592 | tf_op jit(solution)/shard_map/psum | solution.py:102
  248.2 2.3 broadcast_multiply_fusion
  250.5 68.9 %reduce-scatter.5.cloned.1.call-done = bf16[256,512]{1,0:T(8,128)(2,1)} async-done(((bf16[2048,512]{1,0:T(8,128)(2,1)}), bf16[256,512]{1,0:T(8,128)(2,1)}) %reduce-scatter.5.cloned.1.call-update) | async-done | bytes 262160 | tf_op jit(solution)/shard_map/reduce_scatter | solution.py:106
Async XLA Ops:
  7.2 84.5 %copy-start = (bf16[512,512]{1,0:T(8,128)(2,1)S(1)}, bf16[512,512]{1,0:T(8,128)(2,1)}, u32[]{:S(2)}) copy-start(bf16[512,512]{1,0:T(8,128)(2,1)} %param.8) | copy-start | bytes 1572868
  7.2 54.8 %all-gather.6.cloned.1.call-start = ((), (), s32[]{:S(2)}) async-start(), calls=%async_computation.6 | async-start | bytes 2359296 | tf_op jit(solution)/shard_map/all_gather | solution.py:89
  7.9 83.7 %reduce-scatter.3.cloned.1.call-start = ((), (), s32[]{:S(2)}) async-start(), calls=%async_computation.2 | async-start | bytes 1310720 | tf_op jit(solution)/shard_map/reduce_scatter | solution.py:93
  62.0 29.7 %copy-start.2 = (bf16[256,512]{1,0:T(8,128)(2,1)S(1)}, bf16[256,512]{1,0:T(8,128)(2,1)}, u32[]{:S(2)}) copy-start(bf16[256,512]{1,0:T(8,128)(2,1)} %param.9) | copy-start | bytes 786436
  68.2 43.8 %all-gather.4.cloned.1.call-start = ((), (), s32[]{:S(2)}) async-start(), calls=%async_computation.4 | async-start | bytes 1310720 | tf_op jit(solution)/shard_map/all_gather | solution.py:100
  91.7 3.5 %copy-start.1 = (bf16[256,512]{1,0:T(8,128)(2,1)S(1)}, bf16[256,512]{1,0:T(8,128)(2,1)}, u32[]{:S(2)}) copy-start(bf16[256,512]{1,0:T(8,128)(2,1)} %reduce-scatter.3.cloned.1.call-done) | copy-start | bytes 786436
  95.1 153.1 %all-reduce.2.cloned.1.call-start = ((), (), s32[]{:S(2)}) async-start(), calls=%async_computation.3 | async-start | bytes 2097152 | tf_op jit(solution)/shard_map/psum | solution.py:102
  96.5 222.9 %reduce-scatter.5.cloned.1.call-start = ((), (), s32[]{:S(2)}) async-start(), calls=%async_computation.5 | async-start | bytes 2359296 | tf_op jit(solution)/shard_map/reduce_scatter | solution.py:106
Sparse Core Ops, SparseCore 0:
  10.1 51.7 all-gather.5
  68.3 23.3 reduce-scatter.2
  95.2 16.6 all-gather.3
  117.6 130.6 all-reduce.1
  252.2 67.1 reduce-scatter.4
where the time goes:
time: 326 us
  waiting for transfers between devices  283 us (87%)
  matrix products  17.1 us (5%)
  between operations  14.5 us (4%)
  Pallas kernels  9.18 us (3%)
    psum x1, waiting for transfers between devices, local(): weight_grad = lax.psum(weight_term, ('node', 'rep')) * scale  130 us
    reduce_scatter x1, waiting for transfers between devices, local(): lax.psum_scatter(terms.reshape(-1, width), 'node', scatter_dimension=0, t...  68.9 us
    all_gather x1, waiting for transfers between devices, local(): gathered = lax.all_gather(features, 'node', axis=0, tiled=False)  44.2 us
    reduce_scatter x1, waiting for transfers between devices, local(): lax.psum_scatter(partial_sum.astype(jnp.bfloat16), 'rep', scatter_dimensi...  23.4 us
    all_gather x1, waiting for transfers between devices, local(): all_grad = lax.all_gather(row_grad, 'rep', axis=0, tiled=True)  15.4 us
    pallas_call x1, Pallas kernels, densify(): pl.pallas_call(functools.partial(densify_kernel, blocks, subs, group), ou...  9.18 us
  transfers between devices with their start and end apart: 5, of which 5 were waited for; matrix products, arithmetic and copies ran while one was open for 3% of the time, Pallas kernels for 3%

commit v1 on v0

v1 whole, which is shorter than its diff:
```python
import functools
import math

import jax
import jax.numpy as jnp
from jax import lax
from jax.experimental import pallas as pl
from jax.experimental.pallas import tpu as pltpu
from jax.sharding import PartitionSpec as P

TB = 128
MESH = pl.DeviceIdType.MESH
BF = jnp.bfloat16
F32 = jnp.float32


def mm(a, b):
    return jnp.dot(a, b, preferred_element_type=F32)


def layer_kernel(
    cfg, key_ref, last_ref, x_ref, w_ref, c_ref, tiles_hbm,
    act_ref, wsum_ref, fg_ref,
    tiles, stage, dense, dense_t, X, part, psend, precv, agg, pre, pg, wt,
    rg, rsb, rrb, tbuf, aggt, wterm, wsend, wa, wb, wbs, wq, wc, wfull,
    tile_sem, gs, gr, ps, pr, as_, ar, rs, rr,
    was, war, wbss, wbr, wcs, wcr, wds, wdr, wes, wer, wfs, wfr,
):
    N, R, G, Q, D, T, cap, blocks, subs, has_t = cfg
    h = N // 2
    rows, F = x_ref.shape
    gw = F // G
    qr = rows // Q
    i = lax.axis_index("node")
    j = lax.axis_index("rep")
    z, x = lax.div(i, 2), lax.rem(i, 2)
    pos = z + x * (N - 1 - 2 * z)

    def node_at(k):
        p = lax.rem(pos + (k + N), N)
        xx = lax.div(p, N // 2)
        return 2 * (p + xx * (N - 1 - 2 * p)) + xx

    right, left = node_at(1), node_at(-1)
    ring_to = (right, left)
    sent = []

    def rcopy(src, dst, ssem, rsem, dev):
        return pltpu.make_async_remote_copy(
            src_ref=src, dst_ref=dst, send_sem=ssem, recv_sem=rsem,
            device_id=dev, device_id_type=MESH,
        )

    def send(src, dst, ssem, rsem, dev):
        c = rcopy(src, dst, ssem, rsem, dev)
        c.start()
        sent.append(c)

    def arrived(dst, ssem, rsem):
        rcopy(dst, dst, ssem, rsem, (i, j)).wait_recv()

    def half(d):
        return range(d * Q // 2, (d + 1) * Q // 2)

    def xat(o, q):
        return pl.ds(pl.multiple_of(o * rows + q * qr, qr), qr)

    per = cap // T
    tile_copies = [
        pltpu.make_async_copy(
            tiles_hbm.at[pl.ds(k * per, per)], tiles.at[pl.ds(k * per, per)], tile_sem.at[k]
        )
        for k in range(T)
    ]
    for c in tile_copies:
        c.start()

    barrier = pltpu.get_barrier_semaphore()
    for k in range(1, N):
        pl.semaphore_signal(barrier, inc=1, device_id=(lax.rem(i + k, N), j), device_id_type=MESH)
    for k in range(1, R):
        pl.semaphore_signal(barrier, inc=1, device_id=(i, lax.rem(j + k, R)), device_id_type=MESH)
    for g in range(G):
        X[g, pl.ds(pl.multiple_of(i * rows, rows), rows), :] = x_ref[:, g * gw:(g + 1) * gw]
    pl.semaphore_wait(barrier, N - 1 + R - 1)

    def gather_send(g, s, q, d):
        o = node_at(-s if d == 0 else s)
        at = xat(o, q)
        src = x_ref.at[pl.ds(q * qr, qr), pl.ds(g * gw, gw)] if s == 0 else X.at[g, at, :]
        send(src, X.at[g, at, :], gs.at[g, s, q, d], gr.at[g, s, q, d], (ring_to[d], j))

    def gather_start(g):
        for q in range(Q):
            for d in range(2):
                gather_send(g, 0, q, d)

    def gather_event(g, s, q):
        for d in range(2):
            if s == h - 1 and q not in half(d):
                continue
            o = node_at(-(s + 1) if d == 0 else s + 1)
            arrived(X.at[g, xat(o, q), :], gs.at[g, s, q, d], gr.at[g, s, q, d])
            if s + 1 < h and (s + 1 < h - 1 or q in half(d)):
                gather_send(g, s + 1, q, d)
        if s == max(h - 2, 0) and q == Q - 1 and g + 1 < G:
            gather_start(g + 1)

    events = [(g, s, q) for g in range(G) for s in range(h) for q in range(Q)]
    events.reverse()

    def event(count=1):
        for _ in range(count):
            if events:
                gather_event(*events.pop())

    gather_start(0)

    wt[...] = w_ref[...].T
    for c in tile_copies:
        c.wait()
    stage[cap] = jnp.zeros((TB, TB), BF)

    def slot_step(p, carry):
        acc, prev = carry
        key = key_ref[p]
        slot = lax.rem(key, cap)
        place = lax.div(key, cap)
        keep = jnp.where(place == prev, 1.0, 0.0).astype(F32)
        acc = acc * keep + tiles[slot].astype(F32)
        stage[p] = acc.astype(BF)
        return acc, place

    npieces = max(1, 3 * Q)
    carry = (jnp.zeros((TB, TB), F32), jnp.int32(-1))
    bounds = [cap * k // npieces for k in range(npieces + 1)]
    for k in range(npieces):
        carry = lax.fori_loop(bounds[k], bounds[k + 1], slot_step, carry)
        if k >= 3 and len(events) > (G - 1) * h * Q + Q:
            event()

    def place_step(o, carry):
        for r in range(blocks):
            for s in range(subs):
                tile = stage[last_ref[(o * blocks + r) * subs + s]]
                at = pl.ds(pl.multiple_of((o * subs + s) * TB, TB), TB)
                dense[r * TB:(r + 1) * TB, at] = tile
                if has_t:
                    dense_t[at, r * TB:(r + 1) * TB] = tile.T
        return carry

    for k in range(4):
        lax.fori_loop(N * k // 4, N * (k + 1) // 4, place_step, 0)
        if len(events) > (G - 1) * h * Q:
            event()
    while len(events) > (G - 1) * h * Q:
        event()

    def part_send(g, k):
        jj = lax.rem(j + k, R)
        psend[g, k - 1] = part[g, jj].astype(BF)
        send(psend.at[g, k - 1], precv.at[g, k - 1], ps.at[g, k - 1], pr.at[g, k - 1], (i, jj))

    def agg_group(g):
        total = part[g, j]
        for k in range(1, R):
            arrived(precv.at[g, k - 1], ps.at[g, k - 1], pr.at[g, k - 1])
            total += precv[g, k - 1].astype(F32)
        agg[:, g * gw:(g + 1) * gw] = total.astype(BF)

    def full_part(g, jj):
        at = pl.ds(pl.multiple_of(jj * rows, rows), rows)
        part[g, jj] = mm(dense[at, :], X[g])

    def block_part(g, offsets, first):
        def one(m, carry):
            at = pl.ds(pl.multiple_of(m * rows, rows), rows)
            total = None if first else part[g, m]
            for k in offsets:
                col = pl.ds(pl.multiple_of(node_at(k) * rows, rows), rows)
                t = mm(dense[at, col], X[g, col, :])
                total = t if total is None else total + t
            part[g, m] = total
            return carry

        lax.fori_loop(0, R, one, 0)

    def own_pre(g):
        t = mm(agg[:, g * gw:(g + 1) * gw], w_ref[g * gw:(g + 1) * gw, :])
        pre[...] = t if g == 0 else pre[...] + t

    for g in range(G):
        if g < G - 1:
            for k in range(1, R):
                full_part(g, lax.rem(j + k, R))
                part_send(g, k)
                event()
            full_part(g, j)
            left_over = (G - 2 - g) * h * Q
            agg_group(g)
            own_pre(g)
            while len(events) > left_over + h * Q - Q:
                event()
        else:
            block_part(g, [0], True)
            for s in range(h):
                while len(events) > (h - 1 - s) * Q:
                    event()
                block_part(g, [-(s + 1), s + 1] if s < h - 1 else [h], False)
            for k in range(1, R):
                part_send(g, k)
            agg_group(g)
            own_pre(g)

    root = math.sqrt(2.0 / math.pi)
    step = 32 if rows % 32 == 0 else rows

    def act_step(b, carry):
        at = pl.ds(pl.multiple_of(b * step, step), step)
        v = pre[at, :]
        v2 = v * v
        t = jnp.tanh(root * (v + 0.044715 * (v2 * v)))
        half_up = 0.5 * (1.0 + t)
        act_ref[at, :] = (v * half_up).astype(BF)
        slope = half_up + (0.5 * v) * (1.0 - t * t) * (root * (1.0 + (3 * 0.044715) * v2))
        pg[at, :] = (c_ref[at, :].astype(F32) * slope).astype(BF)
        return carry

    lax.fori_loop(0, rows // step, act_step, 0)

    for g in range(G):
        rg[g, j] = mm(pg[...], wt[:, g * gw:(g + 1) * gw]).astype(BF)
        for k in range(1, R):
            send(rg.at[g, j], rg.at[g, j], as_.at[g, k - 1], ar.at[g, k - 1], (i, lax.rem(j + k, R)))

    wr = F // R
    mine, par = lax.div(j, 2), lax.rem(j, 2)
    partner = (i, j + 1 - 2 * par)
    pa = min(N, wr // 16)
    pb = N // pa
    ph, pw = wr // pa, F // pb
    M = R // 2

    def weight_terms():
        aggt[...] = agg[...].T

        def one(k, carry):
            at = pl.ds(pl.multiple_of(k * wr, wr), wr)
            t = mm(aggt[at, :], pg[...])
            wterm[k] = t
            wsend[k] = t.astype(BF)
            return carry

        lax.fori_loop(0, R, one, 0)
        for m in range(M):
            send(wsend.at[2 * m + 1 - par], wa.at[m], was.at[m], war.at[m], partner)

    def weight_chip():
        for m in range(M):
            arrived(wa.at[m], was.at[m], war.at[m])
            wterm[2 * m + par] = wterm[2 * m + par] + wa[m].astype(F32)
        for k in range(1, M):
            to = lax.rem(mine + k, M)
            wbs[k - 1] = wterm[2 * to + par].astype(BF)
            send(wbs.at[k - 1], wb.at[k - 1], wbss.at[k - 1], wbr.at[k - 1], (i, 2 * to + par))

    def piece(n):
        return (
            pl.ds(pl.multiple_of(lax.div(n, pb) * ph, ph), ph),
            pl.ds(pl.multiple_of(lax.rem(n, pb) * pw, pw), pw),
        )

    def weight_rep():
        total = wterm[j]
        for k in range(1, M):
            arrived(wb.at[k - 1], wbss.at[k - 1], wbr.at[k - 1])
            total += wb[k - 1].astype(F32)
        wq[...] = total.astype(BF)
        for k in range(1, N):
            n = lax.rem(i + k, N)
            send(wq.at[piece(n)], wc.at[k - 1], wcs.at[k - 1], wcr.at[k - 1], (n, j))

    def weight_node():
        at = piece(i)
        total = wq[at].astype(F32)
        for k in range(1, N):
            arrived(wc.at[k - 1], wcs.at[k - 1], wcr.at[k - 1])
            total += wc[k - 1].astype(F32)
        wfull[(j,) + at] = total.astype(BF)
        for k in range(1, N):
            spot = wfull.at[(j,) + at]
            send(spot, spot, wds.at[k - 1], wdr.at[k - 1], (lax.rem(i + k, N), j))

    def weight_spread():
        for k in range(1, N):
            spot = wfull.at[(j,) + piece(lax.rem(i - k + N, N))]
            arrived(spot, wds.at[k - 1], wdr.at[k - 1])
        quarter = wfull.at[j]
        for k in range(1, M):
            to = 2 * lax.rem(mine + k, M) + par
            send(quarter, quarter, wes.at[k], wer.at[k], (i, to))
        send(quarter, quarter, wes.at[0], wer.at[0], partner)

    def weight_forward():
        for k in range(1, M):
            spot = wfull.at[2 * lax.rem(mine - k + M, M) + par]
            arrived(spot, wes.at[k], wer.at[k])
            send(spot, spot, wfs.at[k - 1], wfr.at[k - 1], partner)

    def weight_end():
        arrived(wfull.at[j + 1 - 2 * par], wes.at[0], wer.at[0])
        for k in range(1, M):
            spot = wfull.at[2 * lax.rem(mine - k + M, M) + 1 - par]
            arrived(spot, wfs.at[k - 1], wfr.at[k - 1])
        wsum_ref[...] = wfull[...]

    side = [weight_end, weight_forward, weight_spread, weight_node, weight_rep, weight_chip]

    def term(g, o):
        at = pl.ds(pl.multiple_of(o * rows, rows), rows)
        grads = rg[g].reshape(R * rows, gw)
        if has_t:
            return mm(dense_t[at, :], grads)
        return lax.dot_general(
            dense[:, at], grads, (((0,), (0,)), ((), ())), preferred_element_type=F32
        )

    pending = {}

    def ring_send(g, s, q, d):
        at = pl.ds(q * qr, qr)
        c = rcopy(
            rsb.at[g, s % D, d, at, :], rrb.at[g, s, d, at, :],
            rs.at[g, s, q, d], rr.at[g, s, q, d], (ring_to[d], j),
        )
        c.start()
        pending[(g, s, q, d)] = c

    def ring_event(g, s):
        if s == 0:
            tbuf[0] = term(g, node_at(h))
        else:
            for d in range(2):
                tbuf[d] = term(g, node_at(h - s if d == 0 else s - h))
        for q in range(Q):
            at = slice(q * qr, (q + 1) * qr)
            for d in range(2):
                if s == 0 and q not in half(d):
                    continue
                v = tbuf[0 if s == 0 else d, at, :]
                if s > 1 or (s == 1 and q in half(d)):
                    arrived(rrb.at[g, s - 1, d, pl.ds(q * qr, qr), :], rs.at[g, s - 1, q, d], rr.at[g, s - 1, q, d])
                    v += rrb[g, s - 1, d, at, :].astype(F32)
                if (g, s - D, q, d) in pending:
                    pending.pop((g, s - D, q, d)).wait_send()
                rsb[g, s % D, d, at, :] = v.astype(BF)
                ring_send(g, s, q, d)

    def ring_end(g):
        tbuf[0] = term(g, i)
        for q in range(Q):
            at = slice(q * qr, (q + 1) * qr)
            v = tbuf[0, at, :]
            for d in range(2):
                arrived(rrb.at[g, h - 1, d, pl.ds(q * qr, qr), :], rs.at[g, h - 1, q, d], rr.at[g, h - 1, q, d])
                v += rrb[g, h - 1, d, at, :].astype(F32)
            fg_ref[at, g * gw:(g + 1) * gw] = v.astype(BF)

    weight_terms()
    for g in range(G):
        for k in range(1, R):
            spot = rg.at[g, lax.rem(j - k + R, R)]
            arrived(spot, as_.at[g, k - 1], ar.at[g, k - 1])
        for s in range(h):
            ring_event(g, s)
            if s > 0 and len(side) > 1:
                side.pop()()
        if g == G - 1:
            while len(side) > 1:
                side.pop()()
        ring_end(g)
    side.pop()()

    for c in sent:
        c.wait_send()
    for c in pending.values():
        c.wait_send()


def plan_slots(tile_row, tile_col, tile_count, nodes, blocks, subs):
    cap = tile_row.shape[0]
    places = nodes * blocks * subs
    slot = jnp.arange(cap, dtype=jnp.int32)
    place = (tile_col // subs * blocks + tile_row) * subs + tile_col % subs
    place = jnp.where(slot < tile_count[0], place, places)
    key = place * cap + slot
    rank = jnp.sum((key[None, :] < key[:, None]).astype(jnp.int32), axis=1)
    sorted_key = jnp.sum(jnp.where(rank[None, :] == slot[:, None], key[None, :], 0), axis=1)
    spot = jnp.arange(places, dtype=jnp.int32)
    upto = jnp.sum((place[None, :] <= spot[:, None]).astype(jnp.int32), axis=1)
    there = jnp.sum((place[None, :] == spot[:, None]).astype(jnp.int32), axis=1)
    last = jnp.where(there > 0, upto - 1, cap)
    return sorted_key, last


def local(N, R, features, weight, cotangent, tile_values, tile_row, tile_col, tile_count):
    rows, F = features.shape
    cap = tile_values.shape[0]
    subs = rows // TB
    blocks = subs * R
    G, Q, T = 2, 4, 4
    gw, h = F // G, N // 2
    D = min(h, 4)
    qr = rows // Q
    wr = F // R
    pa = min(N, wr // 16)
    ph, pw = wr // pa, F // (N // pa)
    M = R // 2
    has_t = N * rows * rows * R * 2 <= 8 * 1024 * 1024
    sorted_key, last = plan_slots(tile_row, tile_col, tile_count, N, blocks, subs)
    cfg = (N, R, G, Q, D, T, cap, blocks, subs, has_t)
    dma = pltpu.SemaphoreType.DMA
    V = pltpu.VMEM
    scratch = [
        V((cap, TB, TB), BF), V((cap + 1, TB, TB), BF),
        V((R * rows, N * rows), BF),
        V((N * rows, R * rows) if has_t else (16, TB), BF),
        V((G, N * rows, gw), BF), V((G, R, rows, gw), F32),
        V((G, R - 1, rows, gw), BF), V((G, R - 1, rows, gw), BF),
        V((rows, F), BF), V((rows, F), F32), V((rows, F), BF), V((F, F), BF),
        V((G, R, rows, gw), BF), V((G, D, 2, rows, gw), BF), V((G, h, 2, rows, gw), BF),
        V((2, rows, gw), F32), V((F, rows), BF),
        V((R, wr, F), F32), V((R, wr, F), BF), V((M, wr, F), BF),
        V((max(M - 1, 1), wr, F), BF), V((max(M - 1, 1), wr, F), BF),
        V((wr, F), BF), V((N - 1, ph, pw), BF), V((R, wr, F), BF),
        dma((T,)), dma((G, h, Q, 2)), dma((G, h, Q, 2)),
        dma((G, R - 1)), dma((G, R - 1)), dma((G, R - 1)), dma((G, R - 1)),
        dma((G, h, Q, 2)), dma((G, h, Q, 2)),
        dma((M,)), dma((M,)), dma((M,)), dma((M,)),
        dma((N - 1,)), dma((N - 1,)), dma((N - 1,)), dma((N - 1,)),
        dma((M,)), dma((M,)), dma((M,)), dma((M,)),
    ]
    smem = pl.BlockSpec(memory_space=pltpu.SMEM)
    vmem = pl.BlockSpec(memory_space=pltpu.VMEM)
    act, wsum, feature_grad = pl.pallas_call(
        functools.partial(layer_kernel, cfg),
        out_shape=(
            jax.ShapeDtypeStruct((rows, F), BF),
            jax.ShapeDtypeStruct((R, wr, F), BF),
            jax.ShapeDtypeStruct((rows, F), BF),
        ),
        in_specs=[smem, smem, vmem, vmem, vmem, pl.BlockSpec(memory_space=pl.ANY)],
        out_specs=(vmem, vmem, vmem),
        scratch_shapes=scratch,
        compiler_params=pltpu.CompilerParams(
            collective_id=0, has_side_effects=True, vmem_limit_bytes=62 * 1024 * 1024
        ),
        name="layer",
    )(sorted_key, last, features, weight, cotangent, tile_values)
    scale = 1.0 / math.sqrt(rows * R * N)
    weight_grad = wsum.reshape(F, F).astype(F32) * scale
    return act, weight_grad, feature_grad


def solution(mesh):
    in_specs = (
        P(("node", "rep"), None),
        P(),
        P(("node", "rep"), None),
        P(("node", "rep"), None, None),
        P(("node", "rep")),
        P(("node", "rep")),
        P(("node", "rep")),
    )
    out_specs = (P(("node", "rep"), None), P(), P(("node", "rep"), None))
    step = functools.partial(local, mesh.shape["node"], mesh.shape["rep"])
    return jax.shard_map(step, mesh=mesh, in_specs=in_specs, out_specs=out_specs, check_vma=False)
```

time: 326 us -> 96.8 us (0.30)
  waiting for transfers between devices: 283 us -> 0 us
  Pallas kernels: 9.18 us -> 87.4 us
  matrix products: 17.1 us -> 0 us
  between operations: 14.5 us -> 1.29 us
  local copies, waits for them, and re-layouts: 0.02 us -> 3.34 us
    psum x1 -> x0, waiting for transfers between devices: 130 us -> none  [local(): weight_grad = lax.psum(weight_term, ('node', 'rep')) * scale]
    reduce_scatter x2 -> x0, waiting for transfers between devices: 92.3 us -> none  [the longest x1 68.9 us: local(): lax.psum_scatter(terms.reshape(-1, width), 'node', scatter_dimension=0, t...]
    pallas_call x1, Pallas kernels: 9.18 us -> 87.4 us  [local(): pl.pallas_call(functools.partial(layer_kernel, cfg), out_shape=(jax.Shape...]
    all_gather x2 -> x0, waiting for transfers between devices: 59.6 us -> none  [the longest x1 44.2 us: local(): gathered = lax.all_gather(features, 'node', axis=0, tiled=False)]
    dot_general x5 -> x0, matrix products: 17.1 us -> none  [the longest x1 6.19 us: local(): lax.dot_general(dense, all_grad, (((1,), (0,)), ((), ())), preferred_elem...]
    unnamed x6 -> x2, local copies, waits for them, and re-layouts: 0.02 us -> 3.34 us
  transfers between devices with their start and end apart: 5 -> 0, of which waited for: 5 -> 0; matrix products, arithmetic and copies ran while one was open for 3% -> 0% of each run, Pallas kernels for 3% -> 0%
where the time goes in v1:
time: 96.8 us; the launch traced here: 96.4 us
  Pallas kernels  87.4 us (90%)
  other arithmetic  4.37 us (5%)
  local copies, waits for them, and re-layouts  3.34 us (3%)
  between operations  1.29 us (1%)
    pallas_call x1, Pallas kernels, local(): pl.pallas_call(functools.partial(layer_kernel, cfg), out_shape=(jax.Shape...  87.4 us
    unnamed x2, local copies, waits for them, and re-layouts  3.34 us
    mul x1, other arithmetic, local(): weight_grad = wsum.reshape(F, F).astype(F32) * scale  2.16 us

profile of v1, /device:TPU:0, one launch (start us, length us, event | category | flops | bytes accessed | tf_op | source)
XLA Modules:
  0.0 96.4 jit_solution(12652426430449648988)
XLA Ops:
  1.3 0.7 iota_add_fusion
  2.0 0.1 convert_reduce_fusion.1
  2.1 0.5 compare_select_fusion.last_ref
  2.6 0.2 convert_reduce_fusion
  2.8 0.7 select_reduce_fusion.key_ref
  3.5 87.4 %layer.1 = (bf16[256,512]{1,0:T(8,128)(2,1)}, bf16[4,128,512]{2,1,0:T(8,128)(2,1)}, bf16[256,512]{1,0:T(8,128)(2,1)}) custom-call(s32[256]{0:T(256)} %select_reduce_fusion.key_ref, s32[128]{0:T(128)} %compare_select_fusion.last_ref, bf16[256,512]{1,0:T(8,128)(2,1)} %x_ref.1, bf16[512,512]{1,0:T(8,128)(2,1)} %w_ref.1, bf16[256,512]{1,0:T(8,128)(2,1)} %c_ref.1, ...), custom_call_target="tpu_custom_call" | custom-call | tf_op jit(solution)/shard_map/layer/pallas_call | solution.py:445
  90.9 2.2 %convert_multiply_fusion = f32[4,128,512]{2,1,0:T(8,128)} fusion(bf16[4,128,512]{2,1,0:T(8,128)(2,1)} %get-tuple-element.7), kind=kLoop, calls=%fused_computation | loop fusion | flops 524288 | bytes 1572864 | tf_op jit(solution)/shard_map/mul | solution.py:461
  93.1 1.7 %copy.13 = bf16[256,512]{1,0:T(8,128)(2,1)} copy(bf16[256,512]{1,0:T(8,128)(2,1)} %get-tuple-element.16) | data formatting | bytes 524288
  94.7 1.7 %copy.14 = bf16[256,512]{1,0:T(8,128)(2,1)} copy(bf16[256,512]{1,0:T(8,128)(2,1)} %get-tuple-element.18) | data formatting | bytes 524288

commit v2 on v1

v2 whole, which is shorter than its diff:
```python
import functools
import math

import jax
import jax.numpy as jnp
from jax import lax
from jax.experimental import pallas as pl
from jax.experimental.pallas import tpu as pltpu
from jax.sharding import PartitionSpec as P

TB = 128
MESH = pl.DeviceIdType.MESH
BF = jnp.bfloat16
F32 = jnp.float32


def mm(a, b):
    return jnp.dot(a, b, preferred_element_type=F32)


def layer_kernel(
    cfg, count_ref, row_hbm, col_hbm, x_hbm, w_hbm, c_hbm, tiles_hbm,
    act_ref, wsum_ref, fg_ref,
    row_ref, col_ref, tiles, stage, dense, dense_t, X, part, psend, p1, p2s, p2, agg, pre, pg, w_ref, wt, c_ref,
    rg, rsb, rrb, tbuf, aggt, wterm, wsend, wa, wb, wbs, wq, wc, wfull,
    key_v, last_v, key_ref, last_ref,
    in_sem, tile_sem, plan_sem, gs, gr, p1s, p1r, p2ss, p2r, as_, ar, fs, fr, rs, rr,
    was, war, wbss, wbr, wcs, wcr, wds, wdr, wes, wer, wfs, wfr,
):
    N, R, G, D, T, cap, blocks, subs, has_t = cfg
    h, M = N // 2, R // 2
    rows, F = act_ref.shape
    gw = F // G
    hr, hw = rows // 2, gw // 2
    Q = 4
    i = lax.axis_index("node")
    j = lax.axis_index("rep")
    mine, par = lax.div(j, 2), lax.rem(j, 2)
    partner = (i, j + 1 - 2 * par)
    z, x = lax.div(i, 2), lax.rem(i, 2)
    pos = z + x * (N - 1 - 2 * z)

    def node_at(k):
        p = lax.rem(pos + (k + N), N)
        xx = lax.div(p, N // 2)
        return 2 * (p + xx * (N - 1 - 2 * p)) + xx

    right, left = node_at(1), node_at(-1)
    ring_to = (right, left)
    sent = []

    def rcopy(src, dst, ssem, rsem, dev):
        return pltpu.make_async_remote_copy(
            src_ref=src, dst_ref=dst, send_sem=ssem, recv_sem=rsem,
            device_id=dev, device_id_type=MESH,
        )

    def send(src, dst, ssem, rsem, dev):
        c = rcopy(src, dst, ssem, rsem, dev)
        c.start()
        sent.append(c)

    def arrived(dst, ssem, rsem):
        rcopy(dst, dst, ssem, rsem, (i, j)).wait_recv()

    def peer(k):
        return 2 * lax.rem(mine + k + M, M) + par

    def block(o):
        return pl.ds(pl.multiple_of(o * rows, rows), rows)

    def lanes(a):
        return pl.ds(a * hw, hw)

    def unit(q):
        return pl.ds(q % 2 * hr, hr), lanes(q // 2)

    def unit_of(o, q):
        return pl.ds(pl.multiple_of(o * rows + q % 2 * hr, hr), hr), lanes(q // 2)

    ins = [
        pltpu.make_async_copy(x_hbm.at[:, pl.ds(g * gw, gw)], X.at[g, block(i), :], in_sem.at[g])
        for g in range(G)
    ]
    ins.append(pltpu.make_async_copy(w_hbm, w_ref, in_sem.at[G]))
    ins.append(pltpu.make_async_copy(c_hbm, c_ref, in_sem.at[G + 1]))
    per = cap // T
    tile_copies = [
        pltpu.make_async_copy(
            tiles_hbm.at[pl.ds(k * per, per)], tiles.at[pl.ds(k * per, per)], tile_sem.at[k]
        )
        for k in range(T)
    ]
    spots = [
        pltpu.make_async_copy(row_hbm, row_ref, plan_sem.at[2]),
        pltpu.make_async_copy(col_hbm, col_ref, plan_sem.at[3]),
    ]
    for c in spots + ins + tile_copies:
        c.start()

    barrier = pltpu.get_barrier_semaphore()
    for n in ring_to:
        pl.semaphore_signal(barrier, inc=1, device_id=(n, j), device_id_type=MESH)
    for k in range(1, R):
        pl.semaphore_signal(barrier, inc=1, device_id=(i, lax.rem(j + k, R)), device_id_type=MESH)

    for c in spots:
        c.wait()
    places = N * blocks * subs
    slot_row = lax.broadcasted_iota(jnp.int32, (1, cap), 1)
    col = col_ref[...]
    place_row = (lax.div(col, subs) * blocks + row_ref[...]) * subs + lax.rem(col, subs)
    place_row = jnp.where(slot_row < count_ref[0], place_row, places)
    key_row = (place_row * cap + slot_row).astype(F32)
    down = lax.broadcasted_iota(jnp.int32, (cap, cap), 0)
    across = lax.broadcasted_iota(jnp.int32, (cap, cap), 1)
    keys = jnp.broadcast_to(key_row, (cap, cap))
    place_all = jnp.broadcast_to(place_row.astype(F32), (cap, cap))
    key_col = jnp.sum(jnp.where(down == across, keys, 0.0), axis=1, keepdims=True)
    place_col = jnp.sum(jnp.where(down == across, place_all, 0.0), axis=1, keepdims=True)
    rank = jnp.sum(jnp.where(keys < key_col, 1.0, 0.0), axis=1, keepdims=True)
    key_v[...] = jnp.sum(
        jnp.where(rank == across.astype(F32), key_col, 0.0), axis=0, keepdims=True
    ).astype(jnp.int32)
    spot = lax.broadcasted_iota(jnp.int32, (cap, places), 1).astype(F32)
    upto = jnp.sum(jnp.where(place_col <= spot, 1.0, 0.0), axis=0, keepdims=True)
    there = jnp.sum(jnp.where(place_col == spot, 1.0, 0.0), axis=0, keepdims=True)
    last_v[...] = jnp.where(there > 0.0, upto - 1.0, float(cap)).astype(jnp.int32)
    plan = [
        pltpu.make_async_copy(key_v, key_ref, plan_sem.at[0]),
        pltpu.make_async_copy(last_v, last_ref, plan_sem.at[1]),
    ]
    for c in plan:
        c.start()
    for g in range(G):
        ins[g].wait()
    pl.semaphore_wait(barrier, 2 + R - 1)

    def gather_send(g, s, q, d):
        at = (g,) + unit_of(node_at(-s if d == 0 else s), q)
        send(X.at[at], X.at[at], gs.at[g, s, q, d], gr.at[g, s, q, d], (ring_to[d], j))

    fresh = [[(g, q) for g in range(1, G) for q in range(Q)] for d in range(2)]

    def gather_event(g, s, q):
        for d in range(2):
            if s == h - 1 and q % 2 != d:
                continue
            at = (g,) + unit_of(node_at(-(s + 1) if d == 0 else s + 1), q)
            arrived(X.at[at], gs.at[g, s, q, d], gr.at[g, s, q, d])
            if s + 1 < h - 1 or (s + 1 == h - 1 and q % 2 == d):
                gather_send(g, s + 1, q, d)
            elif fresh[d]:
                fg, fq = fresh[d].pop(0)
                gather_send(fg, 0, fq, d)

    events = [(g, s, q) for g in range(G) for s in range(h) for q in range(Q)]
    events.reverse()

    def event_until(left):
        while len(events) > left:
            gather_event(*events.pop())

    for q in range(Q):
        for d in range(2):
            gather_send(0, 0, q, d)

    for c in ins[G:] + tile_copies + plan:
        c.wait()
    wt[...] = w_ref[...].T
    stage[cap] = jnp.zeros((TB, TB), BF)

    def slot_step(p, carry):
        acc, prev = carry
        key = jnp.maximum(key_ref[0, p], 0)
        slot = lax.rem(key, cap)
        place = lax.div(key, cap)
        keep = jnp.where(place == prev, 1.0, 0.0).astype(F32)
        acc = acc * keep + tiles[slot].astype(F32)
        stage[p] = acc.astype(BF)
        return acc, place

    group0 = (G - 1) * h * Q
    carry = (jnp.zeros((TB, TB), F32), jnp.int32(-1))
    for k in range(4):
        carry = lax.fori_loop(cap * k // 4, cap * (k + 1) // 4, slot_step, carry)
        event_until(max(group0, len(events) - 2))

    def place_step(o, carry):
        for r in range(blocks):
            for s in range(subs):
                tile = stage[jnp.clip(last_ref[0, (o * blocks + r) * subs + s], 0, cap)]
                at = pl.ds(pl.multiple_of((o * subs + s) * TB, TB), TB)
                dense[r * TB:(r + 1) * TB, at] = tile
                if has_t:
                    dense_t[at, r * TB:(r + 1) * TB] = tile.T
        return carry

    for k in range(2):
        lax.fori_loop(N * k // 2, N * (k + 1) // 2, place_step, 0)
        event_until(max(group0, len(events) - 2))
    event_until(group0)

    def chip_send(g, a, m, value):
        psend[g, m, :, a * hw:(a + 1) * hw] = value.astype(BF)
        at = (g, m, slice(None), lanes(a))
        send(psend.at[at], p1.at[at], p1s.at[g, a, m], p1r.at[g, a, m], partner)

    def chip_sum(g, a):
        at = slice(a * hw, (a + 1) * hw)
        for k in range(M - 1, -1, -1):
            m = lax.rem(mine + k, M)
            spot = p1.at[g, m, :, lanes(a)]
            arrived(spot, p1s.at[g, a, m], p1r.at[g, a, m])
            total = part[g, 2 * m + par, :, at] + p1[g, m, :, at].astype(F32)
            if k:
                p2s[g, k - 1, :, at] = total.astype(BF)
                spot = (g, k - 1, slice(None), lanes(a))
                send(p2s.at[spot], p2.at[spot], p2ss.at[g, a, k - 1], p2r.at[g, a, k - 1], (i, peer(k)))
            else:
                part[g, j, :, at] = total

    def rep_sum(g, a):
        at = slice(a * hw, (a + 1) * hw)
        total = part[g, j, :, at]
        for k in range(1, M):
            arrived(p2.at[g, k - 1, :, lanes(a)], p2ss.at[g, a, k - 1], p2r.at[g, a, k - 1])
            total += p2[g, k - 1, :, at].astype(F32)
        cols = slice(g * gw + a * hw, g * gw + (a + 1) * hw)
        agg[:, cols] = total.astype(BF)
        t = mm(agg[:, cols], w_ref[cols, :])
        pre[...] = t if g == 0 and a == 0 else pre[...] + t

    def block_part(g, offsets, first):
        def one(m, carry):
            total = None if first else part[g, m]
            for k in offsets:
                cols = block(node_at(k))
                t = mm(dense[block(m), cols], X[g, cols, :])
                total = t if total is None else total + t
            part[g, m] = total
            return carry

        lax.fori_loop(0, R, one, 0)

    for g in range(G):
        end = (G - 1 - g) * h * Q
        if g < G - 1:
            for m in range(M):
                jj = 2 * m + 1 - par
                value = mm(dense[block(jj), :], X[g])
                for a in range(2):
                    chip_send(g, a, m, value[:, a * hw:(a + 1) * hw])
                event_until(len(events) - 1)
            for m in range(M):
                jj = 2 * m + par
                part[g, jj] = mm(dense[block(jj), :], X[g])
                event_until(len(events) - 1)
            for a in range(2):
                chip_sum(g, a)
        else:
            block_part(g, [0], True)
            for s in range(h - 1):
                event_until((h - 1 - s) * Q)
                block_part(g, [-(s + 1), s + 1], False)
                if s == h - 2 and g > 0:
                    for a in range(2):
                        rep_sum(g - 1, a)
            cols = block(node_at(h))
            for a in range(2):
                at = slice(a * hw, (a + 1) * hw)
                event_until((1 - a) * Q // 2)
                for m in range(M):
                    jj = 2 * m + 1 - par
                    chip_send(g, a, m, part[g, jj, :, at] + mm(dense[block(jj), cols], X[g, cols, at]))
                for m in range(M):
                    jj = 2 * m + par
                    part[g, jj, :, at] = part[g, jj, :, at] + mm(dense[block(jj), cols], X[g, cols, at])
            for a in range(2):
                chip_sum(g, a)
            for a in range(2):
                rep_sum(g, a)

    root = math.sqrt(2.0 / math.pi)
    step = 64 if rows % 64 == 0 else rows

    def act_step(b, carry):
        at = pl.ds(pl.multiple_of(b * step, step), step)
        v = pre[at, :]
        v2 = v * v
        t = jnp.tanh(root * (v + 0.044715 * (v2 * v)))
        half_up = 0.5 * (1.0 + t)
        act_ref[at, :] = (v * half_up).astype(BF)
        slope = half_up + (0.5 * v) * (1.0 - t * t) * (root * (1.0 + (3 * 0.044715) * v2))
        pg[at, :] = (c_ref[at, :].astype(F32) * slope).astype(BF)
        return carry

    lax.fori_loop(0, rows // step, act_step, 0)

    def grad_at(g, jj, a):
        return rg.at[g, jj, :, lanes(a)]

    for g in range(G):
        for a in range(2):
            cols = slice(g * gw + a * hw, g * gw + (a + 1) * hw)
            rg[g, j, :, a * hw:(a + 1) * hw] = mm(pg[...], wt[:, cols]).astype(BF)
            spot = grad_at(g, j, a)
            for k in range(1, M):
                send(spot, spot, as_.at[g, a, k], ar.at[g, a, k], (i, peer(k)))
            send(spot, spot, as_.at[g, a, 0], ar.at[g, a, 0], partner)

    def grad_forward(g, a):
        for k in range(1, M):
            spot = grad_at(g, peer(-k), a)
            arrived(spot, as_.at[g, a, k], ar.at[g, a, k])
            send(spot, spot, fs.at[g, a, k - 1], fr.at[g, a, k - 1], partner)

    def grad_ready(g, a):
        arrived(grad_at(g, j + 1 - 2 * par, a), as_.at[g, a, 0], ar.at[g, a, 0])
        for k in range(1, M):
            spot = grad_at(g, peer(-k) + 1 - 2 * par, a)
            arrived(spot, fs.at[g, a, k - 1], fr.at[g, a, k - 1])

    wr = F // R
    pa = min(N, wr // 16)
    pb = N // pa
    ph, pw = wr // pa, F // pb

    def weight_terms():
        aggt[...] = agg[...].T

        def one(k, carry):
            at = pl.ds(pl.multiple_of(k * wr, wr), wr)
            t = mm(aggt[at, :], pg[...])
            wterm[k] = t
            wsend[k] = t.astype(BF)
            return carry

        lax.fori_loop(0, R, one, 0)
        for m in range(M):
            send(wsend.at[2 * m + 1 - par], wa.at[m], was.at[m], war.at[m], partner)

    def weight_chip():
        for m in range(M):
            arrived(wa.at[m], was.at[m], war.at[m])
            wterm[2 * m + par] = wterm[2 * m + par] + wa[m].astype(F32)
        for k in range(1, M):
            to = lax.rem(mine + k, M)
            wbs[k - 1] = wterm[2 * to + par].astype(BF)
            send(wbs.at[k - 1], wb.at[k - 1], wbss.at[k - 1], wbr.at[k - 1], (i, 2 * to + par))

    def piece(n):
        return (
            pl.ds(pl.multiple_of(lax.div(n, pb) * ph, ph), ph),
            pl.ds(pl.multiple_of(lax.rem(n, pb) * pw, pw), pw),
        )

    def weight_rep():
        total = wterm[j]
        for k in range(1, M):
            arrived(wb.at[k - 1], wbss.at[k - 1], wbr.at[k - 1])
            total += wb[k - 1].astype(F32)
        wq[...] = total.astype(BF)
        for k in range(1, N):
            n = lax.rem(i + k, N)
            send(wq.at[piece(n)], wc.at[k - 1], wcs.at[k - 1], wcr.at[k - 1], (n, j))

    def weight_node():
        at = piece(i)
        total = wq[at].astype(F32)
        for k in range(1, N):
            arrived(wc.at[k - 1], wcs.at[k - 1], wcr.at[k - 1])
            total += wc[k - 1].astype(F32)
        wfull[(j,) + at] = total.astype(BF)
        for k in range(1, N):
            spot = wfull.at[(j,) + at]
            send(spot, spot, wds.at[k - 1], wdr.at[k - 1], (lax.rem(i + k, N), j))

    def weight_spread():
        for k in range(1, N):
            spot = wfull.at[(j,) + piece(lax.rem(i - k + N, N))]
            arrived(spot, wds.at[k - 1], wdr.at[k - 1])
        quarter = wfull.at[j]
        for k in range(1, M):
            to = 2 * lax.rem(mine + k, M) + par
            send(quarter, quarter, wes.at[k], wer.at[k], (i, to))
        send(quarter, quarter, wes.at[0], wer.at[0], partner)

    def weight_forward():
        for k in range(1, M):
            spot = wfull.at[2 * lax.rem(mine - k + M, M) + par]
            arrived(spot, wes.at[k], wer.at[k])
            send(spot, spot, wfs.at[k - 1], wfr.at[k - 1], partner)

    def weight_end():
        arrived(wfull.at[j + 1 - 2 * par], wes.at[0], wer.at[0])
        for k in range(1, M):
            spot = wfull.at[2 * lax.rem(mine - k + M, M) + 1 - par]
            arrived(spot, wfs.at[k - 1], wfr.at[k - 1])
        wsum_ref[...] = wfull[...]

    side = [weight_end, weight_forward, weight_spread, weight_node, weight_rep, weight_chip]

    def term(g, o, at):
        grads = rg[g, :, :, at]
        grads = grads.reshape(R * rows, grads.shape[-1])
        if has_t:
            return mm(dense_t[block(o), :], grads)
        return lax.dot_general(
            dense[:, block(o)], grads, (((0,), (0,)), ((), ())), preferred_element_type=F32
        )

    pending = {}

    def ring_send(g, s, q, d):
        at = unit(q)
        c = rcopy(
            rsb.at[(g, s % D, d) + at], rrb.at[(g, s, d) + at],
            rs.at[g, s, q, d], rr.at[g, s, q, d], (ring_to[d], j),
        )
        c.start()
        pending[(g, s, q, d)] = c

    def cut(q):
        return slice(q % 2 * hr, (q % 2 + 1) * hr), slice(q // 2 * hw, (q // 2 + 1) * hw)

    def ring_unit(g, s, q, d, slot, incoming):
        v = tbuf[(slot,) + cut(q)]
        if incoming:
            arrived(rrb.at[(g, s - 1, d) + unit(q)], rs.at[g, s - 1, q, d], rr.at[g, s - 1, q, d])
            v += rrb[(g, s - 1, d) + cut(q)].astype(F32)
        if (g, s - D, q, d) in pending:
            pending.pop((g, s - D, q, d)).wait_send()
        rsb[(g, s % D, d) + cut(q)] = v.astype(BF)
        ring_send(g, s, q, d)

    def ring_event(g, s):
        if s == 0:
            for a in range(2):
                grad_forward(g, a)
                grad_ready(g, a)
                at = slice(a * hw, (a + 1) * hw)
                tbuf[0, :, at] = term(g, node_at(h), at)
                for d in range(2):
                    ring_unit(g, 0, 2 * a + d, d, 0, False)
            return
        for d in range(2):
            tbuf[d] = term(g, node_at(h - s if d == 0 else s - h), slice(None))
        order = [(q, d) for q in range(Q) for d in range(2)]
        if s == 1:
            order = [(q, d) for q, d in order if q % 2 != d] + [(q, d) for q, d in order if q % 2 == d]
        for q, d in order:
            ring_unit(g, s, q, d, d, s > 1 or q % 2 == d)

    def ring_end(g):
        tbuf[0] = term(g, i, slice(None))
        for q in range(Q):
            v = tbuf[(0,) + cut(q)]
            for d in range(2):
                arrived(rrb.at[(g, h - 1, d) + unit(q)], rs.at[g, h - 1, q, d], rr.at[g, h - 1, q, d])
                v += rrb[(g, h - 1, d) + cut(q)].astype(F32)
            r, c = cut(q)
            fg_ref[r, g * gw + c.start:g * gw + c.stop] = v.astype(BF)

    weight_terms()
    turns = []
    for g in range(G):
        turns += [(2 * (g * (h - 1) + s) + (g % 2), g, s) for s in range(h + 1)]
    turns.sort()
    for t, g, s in turns:
        if s < h:
            ring_event(g, s)
        else:
            ring_end(g)
        if len(side) > 1 and (g > 0 or s in (1, 3)):
            side.pop()()
    while side:
        side.pop()()

    for c in sent:
        c.wait_send()
    for c in pending.values():
        c.wait_send()


def finish_kernel(scale, act_in, wsum_in, fg_in, act_out, wg_out, fg_out, wide, sems):
    copies = [
        pltpu.make_async_copy(act_in, act_out, sems.at[0]),
        pltpu.make_async_copy(fg_in, fg_out, sems.at[1]),
    ]
    for c in copies:
        c.start()
    R, wr, F = wsum_in.shape
    for k in range(R):
        at = slice(k * wr, (k + 1) * wr)
        wide[at, :] = wsum_in[k].astype(F32) * scale
        c = pltpu.make_async_copy(wide.at[at, :], wg_out.at[at, :], sems.at[2 + k])
        c.start()
        copies.append(c)
    for c in copies:
        c.wait()


def local(N, R, features, weight, cotangent, tile_values, tile_row, tile_col, tile_count):
    rows, F = features.shape
    cap = tile_values.shape[0]
    subs = rows // TB
    blocks = subs * R
    G, T, Q = 2, 4, 4
    gw, h, M = F // G, N // 2, R // 2
    D = min(h, 4)
    wr = F // R
    pa = min(N, wr // 16)
    ph, pw = wr // pa, F // (N // pa)
    places = N * blocks * subs
    has_t = N * rows * rows * R * 2 <= 8 * 1024 * 1024
    cfg = (N, R, G, D, T, cap, blocks, subs, has_t)
    dma = pltpu.SemaphoreType.DMA
    V = pltpu.VMEM
    M1 = max(M - 1, 1)
    scratch = [
        V((1, cap), jnp.int32), V((1, cap), jnp.int32),
        V((cap, TB, TB), BF), V((cap + 1, TB, TB), BF),
        V((R * rows, N * rows), BF),
        V((N * rows, R * rows) if has_t else (16, TB), BF),
        V((G, N * rows, gw), BF), V((G, R, rows, gw), F32),
        V((G, M, rows, gw), BF), V((G, M, rows, gw), BF), V((G, M1, rows, gw), BF), V((G, M1, rows, gw), BF),
        V((rows, F), BF), V((rows, F), F32), V((rows, F), BF), V((F, F), BF), V((F, F), BF), V((rows, F), BF),
        V((G, R, rows, gw), BF), V((G, D, 2, rows, gw), BF), V((G, h, 2, rows, gw), BF),
        V((2, rows, gw), F32), V((F, rows), BF),
        V((R, wr, F), F32), V((R, wr, F), BF), V((M, wr, F), BF),
        V((M1, wr, F), BF), V((M1, wr, F), BF),
        V((wr, F), BF), V((N - 1, ph, pw), BF), V((R, wr, F), BF),
        V((1, cap), jnp.int32), V((1, places), jnp.int32),
        pltpu.SMEM((1, cap), jnp.int32), pltpu.SMEM((1, places), jnp.int32),
        dma((G + 2,)), dma((T,)), dma((4,)), dma((G, h, Q, 2)), dma((G, h, Q, 2)),
        dma((G, 2, M)), dma((G, 2, M)), dma((G, 2, M1)), dma((G, 2, M1)),
        dma((G, 2, M)), dma((G, 2, M)), dma((G, 2, M1)), dma((G, 2, M1)),
        dma((G, h, Q, 2)), dma((G, h, Q, 2)),
        dma((M,)), dma((M,)), dma((M,)), dma((M,)),
        dma((N - 1,)), dma((N - 1,)), dma((N - 1,)), dma((N - 1,)),
        dma((M,)), dma((M,)), dma((M,)), dma((M,)),
    ]
    smem = pl.BlockSpec(memory_space=pltpu.SMEM)
    vmem = pl.BlockSpec(memory_space=pltpu.VMEM)
    hbm = pl.BlockSpec(memory_space=pltpu.HBM)
    act, wsum, feature_grad = pl.pallas_call(
        functools.partial(layer_kernel, cfg),
        out_shape=(
            jax.ShapeDtypeStruct((rows, F), BF),
            jax.ShapeDtypeStruct((R, wr, F), BF),
            jax.ShapeDtypeStruct((rows, F), BF),
        ),
        in_specs=[smem] + [hbm] * 6,
        out_specs=(vmem, vmem, vmem),
        scratch_shapes=scratch,
        compiler_params=pltpu.CompilerParams(
            collective_id=0, has_side_effects=True,
            vmem_limit_bytes=(48 if has_t else 62) * 1024 * 1024,
        ),
        name="layer",
    )(
        tile_count,
        *(
            pltpu.with_memory_space_constraint(v, pltpu.HBM)
            for v in (
                tile_row.reshape(1, cap), tile_col.reshape(1, cap),
                features, weight, cotangent, tile_values,
            )
        ),
    )
    scale = 1.0 / math.sqrt(rows * R * N)
    act, weight_grad, feature_grad = pl.pallas_call(
        functools.partial(finish_kernel, scale),
        out_shape=(
            jax.ShapeDtypeStruct((rows, F), BF),
            jax.ShapeDtypeStruct((F, F), F32),
            jax.ShapeDtypeStruct((rows, F), BF),
        ),
        in_specs=[vmem, vmem, vmem],
        out_specs=(hbm, hbm, hbm),
        scratch_shapes=[V((F, F), F32), dma((2 + R,))],
        compiler_params=pltpu.CompilerParams(vmem_limit_bytes=8 * 1024 * 1024),
        name="finish",
    )(act, wsum, feature_grad)
    return act, weight_grad, feature_grad


def solution(mesh):
    in_specs = (
        P(("node", "rep"), None),
        P(),
        P(("node", "rep"), None),
        P(("node", "rep"), None, None),
        P(("node", "rep")),
        P(("node", "rep")),
        P(("node", "rep")),
    )
    out_specs = (P(("node", "rep"), None), P(), P(("node", "rep"), None))
    step = functools.partial(local, mesh.shape["node"], mesh.shape["rep"])
    return jax.shard_map(step, mesh=mesh, in_specs=in_specs, out_specs=out_specs, check_vma=False)
```

time: 96.8 us -> 83.5 us (0.86)
  Pallas kernels: 87.4 us -> 82.1 us
  other arithmetic: 4.37 us -> 0 us
  local copies, waits for them, and re-layouts: 3.34 us -> 0 us
    pallas_call x1, Pallas kernels: 87.4 us -> 80.9 us  [local(): pl.pallas_call(functools.partial(layer_kernel, cfg), out_shape=(jax.Shape...]
    unnamed x2 -> x0, local copies, waits for them, and re-layouts: 3.34 us -> none
    mul x1 -> x0, other arithmetic: 2.16 us -> none  [local(): weight_grad = wsum.reshape(F, F).astype(F32) * scale]
    pallas_call x0 -> x1, Pallas kernels: none -> 1.19 us  [local(): pl.pallas_call(functools.partial(finish_kernel, scale), out_shape=(jax.Sh...]
    reduce_sum x3 -> x0, other arithmetic: 0.98 us -> none  [the longest x1 0.69 us: plan_slots(): jnp.sum(jnp.where(rank[None, :] == slot[:, None], key[None, :], 0), axis=1)]
where the time goes in v2:
time: 83.5 us; the launch traced here: 83.4 us
  Pallas kernels  82.1 us (98%)
  between operations  1.29 us (2%)
    pallas_call x1, Pallas kernels, local(): pl.pallas_call(functools.partial(layer_kernel, cfg), out_shape=(jax.Shape...  80.9 us

profile of v2, /device:TPU:0, one launch (start us, length us, event | category | flops | bytes accessed | tf_op | source)
XLA Modules:
  0.0 83.4 jit_solution(7493021063474071080)
XLA Ops:
  1.3 80.9 %layer.1 = (bf16[256,512]{1,0:T(8,128)(2,1)S(1)}, bf16[4,128,512]{2,1,0:T(8,128)(2,1)S(1)}, bf16[256,512]{1,0:T(8,128)(2,1)S(1)}) custom-call(s32[1]{0:T(128)S(6)} %copy.10.count_ref, s32[1,256]{1,0:T(1,128)} %bitcast.2, s32[1,256]{1,0:T(1,128)} %bitcast.3, bf16[256,512]{1,0:T(8,128)(2,1)} %x_hbm.1, bf16[512,512]{1,0:T(8,128)(2,1)} %w_hbm.1, ...), custom_call_target="tpu_custom_call" | custom-call | tf_op jit(solution)/shard_map/layer/pallas_call | solution.py:547
  82.2 1.2 %finish.1 = (bf16[256,512]{1,0:T(8,128)(2,1)}, f32[512,512]{1,0:T(8,128)}, bf16[256,512]{1,0:T(8,128)(2,1)}) custom-call(bf16[256,512]{1,0:T(8,128)(2,1)S(1)} %get-tuple-element.6.act_in, bf16[4,128,512]{2,1,0:T(8,128)(2,1)S(1)} %get-tuple-element.7.wsum_in, bf16[256,512]{1,0:T(8,128)(2,1)S(1)} %get-tuple-element.8.fg_in), custom_call_target="tpu_custom_call" | custom-call | tf_op jit(solution)/shard_map/finish/pallas_call | solution.py:573

commit v3 on v2

--- a/solution.py
+++ b/solution.py
@@ -9,6 +9,8 @@
 from jax.sharding import PartitionSpec as P
 
 TB = 128
+FIRST = 2
+SIDE_AT = (4, 12, 20, 25)
 MESH = pl.DeviceIdType.MESH
 BF = jnp.bfloat16
 F32 = jnp.float32
@@ -103,6 +105,49 @@
         pl.semaphore_signal(barrier, inc=1, device_id=(n, j), device_id_type=MESH)
     for k in range(1, R):
         pl.semaphore_signal(barrier, inc=1, device_id=(i, lax.rem(j + k, R)), device_id_type=MESH)
+
+    for g in range(G):
+        ins[g].wait()
+    pl.semaphore_wait(barrier, 2 + R - 1)
+
+    def gather_send(g, s, q, d):
+        at = (g,) + unit_of(node_at(-s if d == 0 else s), q)
+        send(X.at[at], X.at[at], gs.at[g, s, q, d], gr.at[g, s, q, d], (ring_to[d], j))
+
+    order, late = [(0, 0, q) for q in range(Q)], [(g, 0, q) for g in range(1, G) for q in range(Q)]
+    order, late = order + late[:FIRST], late[FIRST:]
+    first, events, n = list(order), [], 0
+    while n < len(order):
+        g, s, q = order[n]
+        out = []
+        if s + 1 < h - 1 or (s + 1 == h - 1 and q % 2 == 0):
+            out.append((g, s + 1, q))
+        if late and n >= 2:
+            out.append(late.pop(0))
+        order += out
+        events.append(((g, s, q), out))
+        n += 1
+    events.reverse()
+
+    def flip(q, d):
+        return q - q % 2 + (q + d) % 2
+
+    def event(count=1):
+        for _ in range(min(count, len(events))):
+            (g, s, q), out = events.pop()
+            for d in range(2):
+                at = (g,) + unit_of(node_at(-(s + 1) if d == 0 else s + 1), flip(q, d))
+                arrived(X.at[at], gs.at[g, s, flip(q, d), d], gr.at[g, s, flip(q, d), d])
+                for to in out:
+                    gather_send(to[0], to[1], flip(to[2], d), d)
+
+    def need(g, s, a):
+        while any(e[0][0] == g and e[0][1] <= s and e[0][2] // 2 in a for e in events):
+            event()
+
+    for g, s, q in first:
+        for d in range(2):
+            gather_send(g, s, flip(q, d), d)
 
     for c in spots:
         c.wait()
@@ -132,39 +177,6 @@
     ]
     for c in plan:
         c.start()
-    for g in range(G):
-        ins[g].wait()
-    pl.semaphore_wait(barrier, 2 + R - 1)
-
-    def gather_send(g, s, q, d):
-        at = (g,) + unit_of(node_at(-s if d == 0 else s), q)
-        send(X.at[at], X.at[at], gs.at[g, s, q, d], gr.at[g, s, q, d], (ring_to[d], j))
-
-    fresh = [[(g, q) for g in range(1, G) for q in range(Q)] for d in range(2)]
-
-    def gather_event(g, s, q):
-        for d in range(2):
-            if s == h - 1 and q % 2 != d:
-                continue
-            at = (g,) + unit_of(node_at(-(s + 1) if d == 0 else s + 1), q)
-            arrived(X.at[at], gs.at[g, s, q, d], gr.at[g, s, q, d])
-            if s + 1 < h - 1 or (s + 1 == h - 1 and q % 2 == d):
-                gather_send(g, s + 1, q, d)
-            elif fresh[d]:
-                fg, fq = fresh[d].pop(0)
-                gather_send(fg, 0, fq, d)
-
-    events = [(g, s, q) for g in range(G) for s in range(h) for q in range(Q)]
-    events.reverse()
-
-    def event_until(left):
-        while len(events) > left:
-            gather_event(*events.pop())
-
-    for q in range(Q):
-        for d in range(2):
-            gather_send(0, 0, q, d)
-
     for c in ins[G:] + tile_copies + plan:
         c.wait()
     wt[...] = w_ref[...].T
@@ -180,11 +192,10 @@
         stage[p] = acc.astype(BF)
         return acc, place
 
-    group0 = (G - 1) * h * Q
     carry = (jnp.zeros((TB, TB), F32), jnp.int32(-1))
     for k in range(4):
         carry = lax.fori_loop(cap * k // 4, cap * (k + 1) // 4, slot_step, carry)
-        event_until(max(group0, len(events) - 2))
+        event()
 
     def place_step(o, carry):
         for r in range(blocks):
@@ -198,8 +209,7 @@
 
     for k in range(2):
         lax.fori_loop(N * k // 2, N * (k + 1) // 2, place_step, 0)
-        event_until(max(group0, len(events) - 2))
-    event_until(group0)
+        event()
 
     def chip_send(g, a, m, value):
         psend[g, m, :, a * hw:(a + 1) * hw] = value.astype(BF)
@@ -243,43 +253,34 @@
 
         lax.fori_loop(0, R, one, 0)
 
+    def last_block(g, a):
+        cols = block(node_at(h))
+        at = slice(a * hw, (a + 1) * hw)
+        need(g, h - 1, (a,))
+        for m in range(M):
+            jj = 2 * m + 1 - par
+            chip_send(g, a, m, part[g, jj, :, at] + mm(dense[block(jj), cols], X[g, cols, at]))
+        for m in range(M):
+            jj = 2 * m + par
+            part[g, jj, :, at] = part[g, jj, :, at] + mm(dense[block(jj), cols], X[g, cols, at])
+
     for g in range(G):
-        end = (G - 1 - g) * h * Q
-        if g < G - 1:
-            for m in range(M):
-                jj = 2 * m + 1 - par
-                value = mm(dense[block(jj), :], X[g])
-                for a in range(2):
-                    chip_send(g, a, m, value[:, a * hw:(a + 1) * hw])
-                event_until(len(events) - 1)
-            for m in range(M):
-                jj = 2 * m + par
-                part[g, jj] = mm(dense[block(jj), :], X[g])
-                event_until(len(events) - 1)
-            for a in range(2):
-                chip_sum(g, a)
-        else:
-            block_part(g, [0], True)
-            for s in range(h - 1):
-                event_until((h - 1 - s) * Q)
-                block_part(g, [-(s + 1), s + 1], False)
-                if s == h - 2 and g > 0:
-                    for a in range(2):
-                        rep_sum(g - 1, a)
-            cols = block(node_at(h))
-            for a in range(2):
-                at = slice(a * hw, (a + 1) * hw)
-                event_until((1 - a) * Q // 2)
-                for m in range(M):
-                    jj = 2 * m + 1 - par
-                    chip_send(g, a, m, part[g, jj, :, at] + mm(dense[block(jj), cols], X[g, cols, at]))
-                for m in range(M):
-                    jj = 2 * m + par
-                    part[g, jj, :, at] = part[g, jj, :, at] + mm(dense[block(jj), cols], X[g, cols, at])
-            for a in range(2):
-                chip_sum(g, a)
-            for a in range(2):
-                rep_sum(g, a)
+        block_part(g, [0], True)
+        event()
+    for s in range(h - 1):
+        for g in range(G):
+            need(g, s, (0, 1))
+            block_part(g, [-(s + 1), s + 1], False)
+    halves = [(g, a) for g in range(G) for a in range(2)]
+    for k, (g, a) in enumerate(halves):
+        last_block(g, a)
+        if k == len(halves) - 2:
+            for done in halves[:-2]:
+                chip_sum(*done)
+    for done in halves[-2:]:
+        chip_sum(*done)
+    for done in halves:
+        rep_sum(*done)
 
     root = math.sqrt(2.0 / math.pi)
     step = 64 if rows % 64 == 0 else rows
@@ -424,55 +425,66 @@
     def cut(q):
         return slice(q % 2 * hr, (q % 2 + 1) * hr), slice(q // 2 * hw, (q // 2 + 1) * hw)
 
-    def ring_unit(g, s, q, d, slot, incoming):
-        v = tbuf[(slot,) + cut(q)]
-        if incoming:
-            arrived(rrb.at[(g, s - 1, d) + unit(q)], rs.at[g, s - 1, q, d], rr.at[g, s - 1, q, d])
-            v += rrb[(g, s - 1, d) + cut(q)].astype(F32)
-        if (g, s - D, q, d) in pending:
-            pending.pop((g, s - D, q, d)).wait_send()
-        rsb[(g, s % D, d) + cut(q)] = v.astype(BF)
-        ring_send(g, s, q, d)
-
-    def ring_event(g, s):
-        if s == 0:
-            for a in range(2):
-                grad_forward(g, a)
-                grad_ready(g, a)
-                at = slice(a * hw, (a + 1) * hw)
-                tbuf[0, :, at] = term(g, node_at(h), at)
-                for d in range(2):
-                    ring_unit(g, 0, 2 * a + d, d, 0, False)
+    made = set()
+
+    def make(g, s, a):
+        key = (g, s, a if s < 2 else 0)
+        if key in made:
             return
+        made.add(key)
+        at = slice(a * hw, (a + 1) * hw) if s < 2 else slice(None)
+        if s == 0 or s == h:
+            tbuf[g, s % 3, 0, :, at] = term(g, node_at(h) if s == 0 else i, at)
+        else:
+            for d in range(2):
+                tbuf[g, s % 3, d, :, at] = term(g, node_at(h - s if d == 0 else s - h), at)
+
+    def come(g, s, q, d):
+        arrived(rrb.at[(g, s, d) + unit(q)], rs.at[g, s, q, d], rr.at[g, s, q, d])
+        return rrb[(g, s, d) + cut(q)].astype(F32)
+
+    def ring_unit(g, s, u):
+        make(g, s, u // 2)
         for d in range(2):
-            tbuf[d] = term(g, node_at(h - s if d == 0 else s - h), slice(None))
-        order = [(q, d) for q in range(Q) for d in range(2)]
-        if s == 1:
-            order = [(q, d) for q, d in order if q % 2 != d] + [(q, d) for q, d in order if q % 2 == d]
-        for q, d in order:
-            ring_unit(g, s, q, d, d, s > 1 or q % 2 == d)
-
-    def ring_end(g):
-        tbuf[0] = term(g, i, slice(None))
-        for q in range(Q):
-            v = tbuf[(0,) + cut(q)]
+            q = flip(u, d)
+            v = tbuf[(g, s % 3, d if s else 0) + cut(q)]
+            if s > 1 or (s == 1 and u % 2 == 0):
+                v += come(g, s - 1, q, d)
+            if (g, s - D, q, d) in pending:
+                pending.pop((g, s - D, q, d)).wait_send()
+            rsb[(g, s % D, d) + cut(q)] = v.astype(BF)
+            ring_send(g, s, q, d)
+
+    def ring_end(g, a):
+        make(g, h, a)
+        for q in (2 * a, 2 * a + 1):
+            v = tbuf[(g, h % 3, 0) + cut(q)]
             for d in range(2):
-                arrived(rrb.at[(g, h - 1, d) + unit(q)], rs.at[g, h - 1, q, d], rr.at[g, h - 1, q, d])
-                v += rrb[(g, h - 1, d) + cut(q)].astype(F32)
+                v += come(g, h - 1, q, d)
             r, c = cut(q)
             fg_ref[r, g * gw + c.start:g * gw + c.stop] = v.astype(BF)
 
     weight_terms()
-    turns = []
+    order = []
     for g in range(G):
-        turns += [(2 * (g * (h - 1) + s) + (g % 2), g, s) for s in range(h + 1)]
-    turns.sort()
-    for t, g, s in turns:
-        if s < h:
-            ring_event(g, s)
-        else:
-            ring_end(g)
-        if len(side) > 1 and (g > 0 or s in (1, 3)):
+        for a in range(2):
+            grad_forward(g, a)
+            grad_ready(g, a)
+            for s in range(2):
+                ring_unit(g, s, 2 * a + s)
+                order.append((g, s, 2 * a + s))
+        if g == 0:
+            side.pop()()
+    n = 0
+    while n < len(order):
+        g, s, u = order[n]
+        if s + 1 < h:
+            ring_unit(g, s + 1, u)
+            order.append((g, s + 1, u))
+        elif all((g, s, u - u % 2 + k) in order[:n + 1] for k in range(2)):
+            ring_end(g, u // 2)
+        n += 1
+        if n in SIDE_AT and len(side) > 1:
             side.pop()()
     while side:
         side.pop()()
@@ -527,7 +539,7 @@
         V((G, M, rows, gw), BF), V((G, M, rows, gw), BF), V((G, M1, rows, gw), BF), V((G, M1, rows, gw), BF),
         V((rows, F), BF), V((rows, F), F32), V((rows, F), BF), V((F, F), BF), V((F, F), BF), V((rows, F), BF),
         V((G, R, rows, gw), BF), V((G, D, 2, rows, gw), BF), V((G, h, 2, rows, gw), BF),
-        V((2, rows, gw), F32), V((F, rows), BF),
+        V((G, 3, 2, rows, gw), F32), V((F, rows), BF),
         V((R, wr, F), F32), V((R, wr, F), BF), V((M, wr, F), BF),
         V((M1, wr, F), BF), V((M1, wr, F), BF),
         V((wr, F), BF), V((N - 1, ph, pw), BF), V((R, wr, F), BF),
@@ -556,7 +568,7 @@
         scratch_shapes=scratch,
         compiler_params=pltpu.CompilerParams(
             collective_id=0, has_side_effects=True,
-            vmem_limit_bytes=(48 if has_t else 62) * 1024 * 1024,
+            vmem_limit_bytes=(48 if has_t else 63) * 1024 * 1024,
         ),
         name="layer",
     )(

time: 83.5 us -> 77.2 us (0.925)
  Pallas kernels: 82.1 us -> 75.7 us
    pallas_call x1, Pallas kernels: 80.9 us -> 74.5 us  [local(): pl.pallas_call(functools.partial(layer_kernel, cfg), out_shape=(jax.Shape...]
where the time goes in v3:
time: 77.2 us; the launch traced here: 77 us
  Pallas kernels  75.7 us (98%)
  between operations  1.29 us (2%)
    pallas_call x1, Pallas kernels, local(): pl.pallas_call(functools.partial(layer_kernel, cfg), out_shape=(jax.Shape...  74.5 us

profile of v3, /device:TPU:0, one launch (start us, length us, event | category | flops | bytes accessed | tf_op | source)
XLA Modules:
  0.0 77.0 jit_solution(5706017424640564564)
XLA Ops:
  1.3 74.5 %layer.1 = (bf16[256,512]{1,0:T(8,128)(2,1)S(1)}, bf16[4,128,512]{2,1,0:T(8,128)(2,1)S(1)}, bf16[256,512]{1,0:T(8,128)(2,1)S(1)}) custom-call(s32[1]{0:T(128)S(6)} %copy.10.count_ref, s32[1,256]{1,0:T(1,128)} %bitcast.2, s32[1,256]{1,0:T(1,128)} %bitcast.3, bf16[256,512]{1,0:T(8,128)(2,1)} %x_hbm.1, bf16[512,512]{1,0:T(8,128)(2,1)} %w_hbm.1, ...), custom_call_target="tpu_custom_call" | custom-call | tf_op jit(solution)/shard_map/layer/pallas_call | solution.py:559
  75.8 1.2 %finish.1 = (bf16[256,512]{1,0:T(8,128)(2,1)}, f32[512,512]{1,0:T(8,128)}, bf16[256,512]{1,0:T(8,128)(2,1)}) custom-call(bf16[256,512]{1,0:T(8,128)(2,1)S(1)} %get-tuple-element.6.act_in, bf16[4,128,512]{2,1,0:T(8,128)(2,1)S(1)} %get-tuple-element.7.wsum_in, bf16[256,512]{1,0:T(8,128)(2,1)S(1)} %get-tuple-element.8.fg_in), custom_call_target="tpu_custom_call" | custom-call | tf_op jit(solution)/shard_map/finish/pallas_call | solution.py:585

commit v4 on v3

--- a/solution.py
+++ b/solution.py
@@ -9,8 +9,8 @@
 from jax.sharding import PartitionSpec as P
 
 TB = 128
-FIRST = 2
-SIDE_AT = (4, 12, 20, 25)
+FIRST = 4
+SIDE_AT = (2, 6, 10, 17, 23)
 MESH = pl.DeviceIdType.MESH
 BF = jnp.bfloat16
 F32 = jnp.float32
@@ -24,10 +24,10 @@
     cfg, count_ref, row_hbm, col_hbm, x_hbm, w_hbm, c_hbm, tiles_hbm,
     act_ref, wsum_ref, fg_ref,
     row_ref, col_ref, tiles, stage, dense, dense_t, X, part, psend, p1, p2s, p2, agg, pre, pg, w_ref, wt, c_ref,
-    rg, rsb, rrb, tbuf, aggt, wterm, wsend, wa, wb, wbs, wq, wc, wfull,
+    rg, rsb, rrb, tbuf, aggt, wterm, wsend, wa, wb, wbs, wxs, wx, wq, wc, wfull,
     key_v, last_v, key_ref, last_ref,
     in_sem, tile_sem, plan_sem, gs, gr, p1s, p1r, p2ss, p2r, as_, ar, fs, fr, rs, rr,
-    was, war, wbss, wbr, wcs, wcr, wds, wdr, wes, wer, wfs, wfr,
+    was, war, wbss, wbr, wxsem, wcs, wcr, wds, wdr, wes, wer, wfs, wfr,
 ):
     N, R, G, D, T, cap, blocks, subs, has_t = cfg
     h, M = N // 2, R // 2
@@ -275,9 +275,9 @@
     for k, (g, a) in enumerate(halves):
         last_block(g, a)
         if k == len(halves) - 2:
-            for done in halves[:-2]:
+            for done in halves[:-1]:
                 chip_sum(*done)
-    for done in halves[-2:]:
+    for done in halves[-1:]:
         chip_sum(*done)
     for done in halves:
         rep_sum(*done)
@@ -323,9 +323,10 @@
             arrived(spot, fs.at[g, a, k - 1], fr.at[g, a, k - 1])
 
     wr = F // R
-    pa = min(N, wr // 16)
-    pb = N // pa
-    ph, pw = wr // pa, F // pb
+    Z, hx = N // 2, wr // 2
+    pa = min(Z, hx // 16)
+    pb = Z // pa
+    ph, pw = hx // pa, F // pb
 
     def weight_terms():
         aggt[...] = agg[...].T
@@ -350,57 +351,77 @@
             wbs[k - 1] = wterm[2 * to + par].astype(BF)
             send(wbs.at[k - 1], wb.at[k - 1], wbss.at[k - 1], wbr.at[k - 1], (i, 2 * to + par))
 
-    def piece(n):
+    across_node = (i + 1 - 2 * x, j)
+
+    def half_rows(b):
+        return pl.ds(pl.multiple_of(b * hx, hx), hx)
+
+    def other(k):
+        return lax.rem(z + k + Z, Z)
+
+    def piece(n, base):
         return (
-            pl.ds(pl.multiple_of(lax.div(n, pb) * ph, ph), ph),
+            pl.ds(pl.multiple_of(base + lax.div(n, pb) * ph, ph), ph),
             pl.ds(pl.multiple_of(lax.rem(n, pb) * pw, pw), pw),
         )
 
     def weight_rep():
-        total = wterm[j]
-        for k in range(1, M):
-            arrived(wb.at[k - 1], wbss.at[k - 1], wbr.at[k - 1])
-            total += wb[k - 1].astype(F32)
-        wq[...] = total.astype(BF)
-        for k in range(1, N):
-            n = lax.rem(i + k, N)
-            send(wq.at[piece(n)], wc.at[k - 1], wcs.at[k - 1], wcr.at[k - 1], (n, j))
+        for b in (1 - x, x):
+            total = wterm[j, half_rows(b), :]
+            for k in range(1, M):
+                if b is not x:
+                    arrived(wb.at[k - 1], wbss.at[k - 1], wbr.at[k - 1])
+                total += wb[k - 1, half_rows(b), :].astype(F32)
+            if b is x:
+                wterm[j, half_rows(b), :] = total
+            else:
+                wxs[...] = total.astype(BF)
+                send(wxs, wx, wxsem.at[0], wxsem.at[1], across_node)
+
+    def weight_pair():
+        arrived(wx, wxsem.at[0], wxsem.at[1])
+        wq[...] = (wterm[j, half_rows(x), :] + wx[...].astype(F32)).astype(BF)
+        for k in range(1, Z):
+            n = other(k)
+            send(wq.at[piece(n, 0)], wc.at[k - 1], wcs.at[k - 1], wcr.at[k - 1], (2 * n + x, j))
 
     def weight_node():
-        at = piece(i)
-        total = wq[at].astype(F32)
-        for k in range(1, N):
+        total = wq[piece(z, 0)].astype(F32)
+        for k in range(1, Z):
             arrived(wc.at[k - 1], wcs.at[k - 1], wcr.at[k - 1])
             total += wc[k - 1].astype(F32)
-        wfull[(j,) + at] = total.astype(BF)
+        at = (j,) + piece(z, x * hx)
+        wfull[at] = total.astype(BF)
         for k in range(1, N):
-            spot = wfull.at[(j,) + at]
-            send(spot, spot, wds.at[k - 1], wdr.at[k - 1], (lax.rem(i + k, N), j))
+            send(wfull.at[at], wfull.at[at], wds.at[k - 1], wdr.at[k - 1], (lax.rem(i + k, N), j))
 
     def weight_spread():
         for k in range(1, N):
-            spot = wfull.at[(j,) + piece(lax.rem(i - k + N, N))]
-            arrived(spot, wds.at[k - 1], wdr.at[k - 1])
-        quarter = wfull.at[j]
+            n = lax.rem(i - k + N, N)
+            at = (j,) + piece(lax.div(n, 2), lax.rem(n, 2) * hx)
+            arrived(wfull.at[at], wds.at[k - 1], wdr.at[k - 1])
+        spot = wfull.at[j]
         for k in range(1, M):
-            to = 2 * lax.rem(mine + k, M) + par
-            send(quarter, quarter, wes.at[k], wer.at[k], (i, to))
-        send(quarter, quarter, wes.at[0], wer.at[0], partner)
+            send(spot, spot, wes.at[k], wer.at[k], (i, peer(k)))
+        send(spot, spot, wes.at[0], wer.at[0], partner)
 
     def weight_forward():
         for k in range(1, M):
-            spot = wfull.at[2 * lax.rem(mine - k + M, M) + par]
+            spot = wfull.at[peer(-k)]
             arrived(spot, wes.at[k], wer.at[k])
             send(spot, spot, wfs.at[k - 1], wfr.at[k - 1], partner)
 
     def weight_end():
         arrived(wfull.at[j + 1 - 2 * par], wes.at[0], wer.at[0])
         for k in range(1, M):
-            spot = wfull.at[2 * lax.rem(mine - k + M, M) + 1 - par]
+            spot = wfull.at[peer(-k) + 1 - 2 * par]
             arrived(spot, wfs.at[k - 1], wfr.at[k - 1])
         wsum_ref[...] = wfull[...]
 
-    side = [weight_end, weight_forward, weight_spread, weight_node, weight_rep, weight_chip]
+    side = [
+        weight_end, weight_forward, weight_spread,
+        weight_node, weight_pair, weight_rep, weight_chip,
+    ]
 
     def term(g, o, at):
         grads = rg[g, :, :, at]
@@ -522,8 +543,9 @@
     gw, h, M = F // G, N // 2, R // 2
     D = min(h, 4)
     wr = F // R
-    pa = min(N, wr // 16)
-    ph, pw = wr // pa, F // (N // pa)
+    Z, hx = N // 2, wr // 2
+    pa = min(Z, hx // 16)
+    ph, pw = hx // pa, F // (Z // pa)
     places = N * blocks * subs
     has_t = N * rows * rows * R * 2 <= 8 * 1024 * 1024
     cfg = (N, R, G, D, T, cap, blocks, subs, has_t)
@@ -542,15 +564,15 @@
         V((G, 3, 2, rows, gw), F32), V((F, rows), BF),
         V((R, wr, F), F32), V((R, wr, F), BF), V((M, wr, F), BF),
         V((M1, wr, F), BF), V((M1, wr, F), BF),
-        V((wr, F), BF), V((N - 1, ph, pw), BF), V((R, wr, F), BF),
+        V((hx, F), BF), V((hx, F), BF), V((hx, F), BF), V((Z - 1, ph, pw), BF), V((R, wr, F), BF),
         V((1, cap), jnp.int32), V((1, places), jnp.int32),
         pltpu.SMEM((1, cap), jnp.int32), pltpu.SMEM((1, places), jnp.int32),
         dma((G + 2,)), dma((T,)), dma((4,)), dma((G, h, Q, 2)), dma((G, h, Q, 2)),
         dma((G, 2, M)), dma((G, 2, M)), dma((G, 2, M1)), dma((G, 2, M1)),
         dma((G, 2, M)), dma((G, 2, M)), dma((G, 2, M1)), dma((G, 2, M1)),
         dma((G, h, Q, 2)), dma((G, h, Q, 2)),
-        dma((M,)), dma((M,)), dma((M,)), dma((M,)),
-        dma((N - 1,)), dma((N - 1,)), dma((N - 1,)), dma((N - 1,)),
+        dma((M,)), dma((M,)), dma((M,)), dma((M,)), dma((2,)),
+        dma((Z - 1,)), dma((Z - 1,)), dma((N - 1,)), dma((N - 1,)),
         dma((M,)), dma((M,)), dma((M,)), dma((M,)),
     ]
     smem = pl.BlockSpec(memory_space=pltpu.SMEM)

time: 77.2 us -> 75.1 us (0.973)
  Pallas kernels: 75.7 us -> 73.7 us
    pallas_call x1, Pallas kernels: 74.5 us -> 72.5 us  [local(): pl.pallas_call(functools.partial(layer_kernel, cfg), out_shape=(jax.Shape...]
where the time goes in v4:
time: 75.1 us; the launch traced here: 74.9 us
  Pallas kernels  73.7 us (98%)
  between operations  1.29 us (2%)
    pallas_call x1, Pallas kernels, local(): pl.pallas_call(functools.partial(layer_kernel, cfg), out_shape=(jax.Shape...  72.5 us

profile of v4, /device:TPU:0, one launch (start us, length us, event | category | flops | bytes accessed | tf_op | source)
XLA Modules:
  0.0 74.9 jit_solution(12422106459059625330)
XLA Ops:
  1.3 72.5 %layer.1 = (bf16[256,512]{1,0:T(8,128)(2,1)S(1)}, bf16[4,128,512]{2,1,0:T(8,128)(2,1)S(1)}, bf16[256,512]{1,0:T(8,128)(2,1)S(1)}) custom-call(s32[1]{0:T(128)S(6)} %copy.10.count_ref, s32[1,256]{1,0:T(1,128)} %bitcast.2, s32[1,256]{1,0:T(1,128)} %bitcast.3, bf16[256,512]{1,0:T(8,128)(2,1)} %x_hbm.1, bf16[512,512]{1,0:T(8,128)(2,1)} %w_hbm.1, ...), custom_call_target="tpu_custom_call" | custom-call | tf_op jit(solution)/shard_map/layer/pallas_call | solution.py:581
  73.8 1.2 %finish.1 = (bf16[256,512]{1,0:T(8,128)(2,1)}, f32[512,512]{1,0:T(8,128)}, bf16[256,512]{1,0:T(8,128)(2,1)}) custom-call(bf16[256,512]{1,0:T(8,128)(2,1)S(1)} %get-tuple-element.6.act_in, bf16[4,128,512]{2,1,0:T(8,128)(2,1)S(1)} %get-tuple-element.7.wsum_in, bf16[256,512]{1,0:T(8,128)(2,1)S(1)} %get-tuple-element.8.fg_in), custom_call_target="tpu_custom_call" | custom-call | tf_op jit(solution)/shard_map/finish/pallas_call | solution.py:607

commit v5 on v4

--- a/solution.py
+++ b/solution.py
@@ -10,7 +10,7 @@
 
 TB = 128
 FIRST = 4
-SIDE_AT = (2, 6, 10, 17, 23)
+SIDE_AT = (1, 5, 9, 17, 23)
 MESH = pl.DeviceIdType.MESH
 BF = jnp.bfloat16
 F32 = jnp.float32
@@ -257,7 +257,8 @@
         cols = block(node_at(h))
         at = slice(a * hw, (a + 1) * hw)
         need(g, h - 1, (a,))
-        for m in range(M):
+        for k in range(M - 1, -1, -1):
+            m = lax.rem(mine + k, M)
             jj = 2 * m + 1 - par
             chip_send(g, a, m, part[g, jj, :, at] + mm(dense[block(jj), cols], X[g, cols, at]))
         for m in range(M):
@@ -486,6 +487,7 @@
             fg_ref[r, g * gw + c.start:g * gw + c.stop] = v.astype(BF)
 
     weight_terms()
+    side.pop()()
     order = []
     for g in range(G):
         for a in range(2):
@@ -494,8 +496,6 @@
             for s in range(2):
                 ring_unit(g, s, 2 * a + s)
                 order.append((g, s, 2 * a + s))
-        if g == 0:
-            side.pop()()
     n = 0
     while n < len(order):
         g, s, u = order[n]

time: 75.1 us -> 74.8 us (level)
  no operation moved by 1% of the time
where the time goes in v5:
time: 74.8 us; the launch traced here: 74.7 us
  Pallas kernels  73.4 us (98%)
  between operations  1.29 us (2%)
    pallas_call x1, Pallas kernels, local(): pl.pallas_call(functools.partial(layer_kernel, cfg), out_shape=(jax.Shape...  72.2 us

profile of v5, /device:TPU:0, one launch (start us, length us, event | category | flops | bytes accessed | tf_op | source)
XLA Modules:
  0.0 74.7 jit_solution(7337526078104369510)
XLA Ops:
  1.3 72.2 %layer.1 = (bf16[256,512]{1,0:T(8,128)(2,1)S(1)}, bf16[4,128,512]{2,1,0:T(8,128)(2,1)S(1)}, bf16[256,512]{1,0:T(8,128)(2,1)S(1)}) custom-call(s32[1]{0:T(128)S(6)} %copy.10.count_ref, s32[1,256]{1,0:T(1,128)} %bitcast.2, s32[1,256]{1,0:T(1,128)} %bitcast.3, bf16[256,512]{1,0:T(8,128)(2,1)} %x_hbm.1, bf16[512,512]{1,0:T(8,128)(2,1)} %w_hbm.1, ...), custom_call_target="tpu_custom_call" | custom-call | tf_op jit(solution)/shard_map/layer/pallas_call | solution.py:581
  73.5 1.2 %finish.1 = (bf16[256,512]{1,0:T(8,128)(2,1)}, f32[512,512]{1,0:T(8,128)}, bf16[256,512]{1,0:T(8,128)(2,1)}) custom-call(bf16[256,512]{1,0:T(8,128)(2,1)S(1)} %get-tuple-element.6.act_in, bf16[4,128,512]{2,1,0:T(8,128)(2,1)S(1)} %get-tuple-element.7.wsum_in, bf16[256,512]{1,0:T(8,128)(2,1)S(1)} %get-tuple-element.8.fg_in), custom_call_target="tpu_custom_call" | custom-call | tf_op jit(solution)/shard_map/finish/pallas_call | solution.py:607

commit v6 on v5

--- a/solution.py
+++ b/solution.py
@@ -10,7 +10,7 @@
 
 TB = 128
 FIRST = 4
-SIDE_AT = (1, 5, 9, 17, 23)
+SIDE_AT = (2, 6, 11, 20, 26)
 MESH = pl.DeviceIdType.MESH
 BF = jnp.bfloat16
 F32 = jnp.float32

time: 74.8 us -> 74.8 us (level)
  no operation moved by 1% of the time
where the time goes in v6:
time: 74.8 us; the launch traced here: 74.7 us
  Pallas kernels  73.4 us (98%)
  between operations  1.29 us (2%)
    pallas_call x1, Pallas kernels, local(): pl.pallas_call(functools.partial(layer_kernel, cfg), out_shape=(jax.Shape...  72.2 us

profile of v6, /device:TPU:0, one launch (start us, length us, event | category | flops | bytes accessed | tf_op | source)
XLA Modules:
  0.0 74.7 jit_solution(135445156169140986)
XLA Ops:
  1.3 72.2 %layer.1 = (bf16[256,512]{1,0:T(8,128)(2,1)S(1)}, bf16[4,128,512]{2,1,0:T(8,128)(2,1)S(1)}, bf16[256,512]{1,0:T(8,128)(2,1)S(1)}) custom-call(s32[1]{0:T(128)S(6)} %copy.10.count_ref, s32[1,256]{1,0:T(1,128)} %bitcast.2, s32[1,256]{1,0:T(1,128)} %bitcast.3, bf16[256,512]{1,0:T(8,128)(2,1)} %x_hbm.1, bf16[512,512]{1,0:T(8,128)(2,1)} %w_hbm.1, ...), custom_call_target="tpu_custom_call" | custom-call | tf_op jit(solution)/shard_map/layer/pallas_call | solution.py:581
  73.5 1.2 %finish.1 = (bf16[256,512]{1,0:T(8,128)(2,1)}, f32[512,512]{1,0:T(8,128)}, bf16[256,512]{1,0:T(8,128)(2,1)}) custom-call(bf16[256,512]{1,0:T(8,128)(2,1)S(1)} %get-tuple-element.6.act_in, bf16[4,128,512]{2,1,0:T(8,128)(2,1)S(1)} %get-tuple-element.7.wsum_in, bf16[256,512]{1,0:T(8,128)(2,1)S(1)} %get-tuple-element.8.fg_in), custom_call_target="tpu_custom_call" | custom-call | tf_op jit(solution)/shard_map/finish/pallas_call | solution.py:607
